TPU v7x, 32 devices: a whole 2x2x4 slice. The times are simulated.
32 devices in a mesh: row: 8 (over y, x, core), col: 4 (over z).
Axes of the slice: x: 2, y: 2, z: 4, core: 2. Of those that a mesh axis runs over, the one named last changes fastest.
Arguments:
- tokens: bfloat16 [2, 8192, 512], P(None, ('row', 'col')), may hold values from -6 to 6
- encoded: bfloat16 [2, 8192, 512], P(None, ('row', 'col')), may hold values from -6 to 6
- source_len: int32 [2, 8], P(None, 'row'), may hold values from 256 to 1024, as said below
- out_grad: float32 [2, 8192, 512], P(None, ('row', 'col')), may hold values from -6 to 6
- self_query: bfloat16 [512, 512], P('row', 'col'), may hold values from -0.25 to 0.25
- self_key: bfloat16 [512, 512], P('row', 'col'), may hold values from -0.25 to 0.25
- self_value: bfloat16 [512, 512], P('row', 'col'), may hold values from -0.25 to 0.25
- self_output: bfloat16 [512, 512], P('col', 'row'), may hold values from -2 to 2
- self_query_bias: float32 [512], replicated, may hold values from -3 to 3
- self_value_bias: float32 [512], replicated, may hold values from -3 to 3
- self_output_bias: float32 [512], replicated, may hold values from -3 to 3
- cross_query: bfloat16 [512, 512], P('row', 'col'), may hold values from -0.25 to 0.25
- cross_key: bfloat16 [512, 512], P('row', 'col'), may hold values from -0.25 to 0.25
- cross_value: bfloat16 [512, 512], P('row', 'col'), may hold values from -0.25 to 0.25
- cross_output: bfloat16 [512, 512], P('col', 'row'), may hold values from -2 to 2
- cross_query_bias: float32 [512], replicated, may hold values from -3 to 3
- cross_value_bias: float32 [512], replicated, may hold values from -3 to 3
- cross_output_bias: float32 [512], replicated, may hold values from -3 to 3
- expand: bfloat16 [512, 2048], P('row', 'col'), may hold values from -0.25 to 0.25
- expand_bias: float32 [2048], replicated, may hold values from -3 to 3
- contract: bfloat16 [2048, 512], P('col', 'row'), may hold values from -0.125 to 0.125
- contract_bias: float32 [512], replicated, may hold values from -3 to 3
- attn_gain: float32 [512], replicated, may hold values from 0.1 to 1.9
- attn_shift: float32 [512], replicated, may hold values from -3 to 3
- cross_gain: float32 [512], replicated, may hold values from 0.1 to 1.9
- cross_shift: float32 [512], replicated, may hold values from -3 to 3
- final_gain: float32 [512], replicated, may hold values from 0.1 to 1.9
- final_shift: float32 [512], replicated, may hold values from -3 to 3
Outputs:
- result: float32 [2, 8192, 512], P(None, ('row', 'col'))
- tokens_grad: float32 [2, 8192, 512], P(None, ('row', 'col'))
- encoded_grad: float32 [2, 8192, 512], P(None, ('row', 'col'))
- self_query_grad: float32 [512, 512], P('row', 'col')
- self_key_grad: float32 [512, 512], P('row', 'col')
- self_value_grad: float32 [512, 512], P('row', 'col')
- self_output_grad: float32 [512, 512], P('col', 'row')
- self_query_bias_grad: float32 [512], replicated
- self_value_bias_grad: float32 [512], replicated
- self_output_bias_grad: float32 [512], replicated
- cross_query_grad: float32 [512, 512], P('row', 'col')
- cross_key_grad: float32 [512, 512], P('row', 'col')
- cross_value_grad: float32 [512, 512], P('row', 'col')
- cross_output_grad: float32 [512, 512], P('col', 'row')
- cross_query_bias_grad: float32 [512], replicated
- cross_value_bias_grad: float32 [512], replicated
- cross_output_bias_grad: float32 [512], replicated
- expand_grad: float32 [512, 2048], P('row', 'col')
- expand_bias_grad: float32 [2048], replicated
- contract_grad: float32 [2048, 512], P('col', 'row')
- contract_bias_grad: float32 [512], replicated
- attn_gain_grad: float32 [512], replicated
- attn_shift_grad: float32 [512], replicated
- cross_gain_grad: float32 [512], replicated
- cross_shift_grad: float32 [512], replicated
- final_gain_grad: float32 [512], replicated
- final_shift_grad: float32 [512], replicated
Inputs may be any that keep to these rules, and one draw needn't show every extreme that they name: `source_len`: every micro-batch has a sequence with all 1024 encoder states and one with 256.
All inputs are finite; a program needn't handle non-finite values.
Results may differ from a plain program's by a relative error of at most 0.022.
The roundings to bfloat16 on the way count: a program that leaves them out, or rounds other values in their place, can miss the bound.
Values may be sent and summed in bfloat16 or wider, within the bound.
A program may use at most 128 MiB of HBM per device.

v0:
```python
import jax
import jax.numpy as jnp
from jax import lax
from jax.sharding import PartitionSpec as P

HEAD_DIM = 64


NEGATIVE = -1e30
EPSILON = 1e-05


def in_blocks(value, dim, peers):
    lengths = value.shape
    blocks = value.reshape(*lengths[:dim], peers, lengths[dim] // peers, *lengths[dim + 1 :])
    return jnp.moveaxis(blocks, dim, 0)


def summed_on_arrival(value, axis, dim):
    peers = lax.axis_size(axis)
    blocks = lax.all_to_all(in_blocks(value, dim, peers), axis, 0, 0, tiled=True)
    return jnp.sum(blocks.astype(jnp.float32), axis=0)


def sent_together(arrays, axis, dim, along):
    widths = [a.shape[along] for a in arrays]
    both = jnp.concatenate(arrays, axis=along)
    result = summed_on_arrival(both, axis, dim)
    return tuple(jnp.split(result, [sum(widths[:k]) for k in range(1, len(widths))], axis=along))


def product(left_side, right_side):
    return jnp.dot(left_side, right_side, preferred_element_type=jnp.float32)


def over_rows(left_side, right_side):
    return lax.dot_general(
        left_side, right_side, (((0,), (0,)), ((), ())), preferred_element_type=jnp.float32
    )


def against(left_side, right_side):
    return lax.dot_general(
        left_side, right_side, (((1,), (1,)), ((), ())), preferred_element_type=jnp.float32
    )


def norm_forward(values, norm_gain, norm_shift):
    average = jnp.mean(values, axis=1, keepdims=True)
    centered = values - average
    inverse = lax.rsqrt(jnp.mean(centered * centered, axis=1, keepdims=True) + EPSILON)
    normed = centered * inverse
    return (normed * norm_gain + norm_shift, normed, inverse)


def norm_backward(gradient, normed, inverse, norm_gain):
    scaled = gradient * norm_gain
    centered = scaled - jnp.mean(scaled, axis=1, keepdims=True)
    centered = centered - normed * jnp.mean(scaled * normed, axis=1, keepdims=True)
    return (centered * inverse, jnp.sum(gradient * normed, axis=0), jnp.sum(gradient, axis=0))


def causal_rule(seq_index, query_pos, key_pos):
    return query_pos[:, None] >= key_pos[None, :]


def source_rule(source_now):

    def allowed(seq_index, query_pos, key_pos):
        limit = lax.dynamic_index_in_dim(source_now, seq_index, 0, keepdims=False)
        return jnp.broadcast_to(key_pos[None, :] < limit, (query_pos.shape[0], key_pos.shape[0]))

    return allowed


def layout(query_rows, key_rows, seq_count):
    length = query_rows.shape[0] // seq_count
    key_span = key_rows.shape[0] // seq_count
    block_rows = min(512, length)
    block_count = length // block_rows
    head_count = query_rows.shape[1] // HEAD_DIM
    return (key_span, block_rows, block_count, head_count)


def attend(query_rows, key_rows, value_rows, seq_count, allowed):
    key_span, block_rows, block_count, head_count = layout(query_rows, key_rows, seq_count)
    query_blocks = query_rows.reshape(seq_count * block_count, block_rows, head_count, HEAD_DIM)
    key_heads = key_rows.reshape(seq_count, key_span, head_count, HEAD_DIM)
    value_heads = value_rows.reshape(seq_count, key_span, head_count, HEAD_DIM)

    def one_block(block_item):
        query_block, block_index = block_item
        seq_index = block_index // block_count
        offset = block_index % block_count * block_rows
        key_block = lax.dynamic_index_in_dim(key_heads, seq_index, 0, keepdims=False)
        value_block = lax.dynamic_index_in_dim(value_heads, seq_index, 0, keepdims=False)
        scores = jnp.einsum(
            "qhd,khd->hqk", query_block, key_block, preferred_element_type=jnp.float32
        )
        permit = allowed(seq_index, offset + jnp.arange(block_rows), jnp.arange(key_span))
        scores = jnp.where(permit[None], scores, NEGATIVE)
        row_max = jnp.max(scores, axis=-1, keepdims=True)
        raised = jnp.exp(scores - row_max)
        summed = jnp.sum(raised, axis=-1, keepdims=True)
        attn_probs = (raised / summed).astype(jnp.bfloat16)
        mixed_heads = jnp.einsum(
            "hqk,khd->qhd", attn_probs, value_block, preferred_element_type=jnp.float32
        )
        return (mixed_heads.astype(jnp.bfloat16), (row_max + jnp.log(summed))[..., 0])

    mixed_heads, log_total = lax.map(one_block, (query_blocks, jnp.arange(seq_count * block_count)))
    return (mixed_heads.reshape(query_rows.shape[0], -1), log_total)


def attend_back(query_rows, key_rows, value_rows, log_total, mixed_grad, seq_count, allowed):
    key_span, block_rows, block_count, head_count = layout(query_rows, key_rows, seq_count)
    query_blocks = query_rows.reshape(seq_count * block_count, block_rows, head_count, HEAD_DIM)
    grad_blocks = mixed_grad.reshape(seq_count * block_count, block_rows, head_count, HEAD_DIM)
    key_heads = key_rows.reshape(seq_count, key_span, head_count, HEAD_DIM)
    value_heads = value_rows.reshape(seq_count, key_span, head_count, HEAD_DIM)
    empty = jnp.zeros((seq_count, key_span, head_count, HEAD_DIM), jnp.float32)

    def one_block(running, block_item):
        key_grads, value_grads = running
        query_block, grad_block, block_stats, block_index = block_item
        seq_index = block_index // block_count
        offset = block_index % block_count * block_rows
        key_block = lax.dynamic_index_in_dim(key_heads, seq_index, 0, keepdims=False)
        value_block = lax.dynamic_index_in_dim(value_heads, seq_index, 0, keepdims=False)
        scores = jnp.einsum(
            "qhd,khd->hqk", query_block, key_block, preferred_element_type=jnp.float32
        )
        permit = allowed(seq_index, offset + jnp.arange(block_rows), jnp.arange(key_span))
        scores = jnp.where(permit[None], scores, NEGATIVE)
        attn_probs = jnp.exp(scores - block_stats[..., None])
        prob_grads = jnp.einsum(
            "qhd,khd->hqk", grad_block, value_block, preferred_element_type=jnp.float32
        )
        score_grads = attn_probs * (
            prob_grads - jnp.sum(prob_grads * attn_probs, axis=-1, keepdims=True)
        )
        score_low = score_grads.astype(jnp.bfloat16)
        query_grad = jnp.einsum(
            "hqk,khd->qhd", score_low, key_block, preferred_element_type=jnp.float32
        )
        key_grad = jnp.einsum(
            "hqk,qhd->khd", score_low, query_block, preferred_element_type=jnp.float32
        )
        value_grad = jnp.einsum(
            "hqk,qhd->khd",
            attn_probs.astype(jnp.bfloat16),
            grad_block,
            preferred_element_type=jnp.float32,
        )
        key_grads = key_grads.at[seq_index].add(key_grad)
        value_grads = value_grads.at[seq_index].add(value_grad)
        return ((key_grads, value_grads), query_grad)

    (key_grads, value_grads), query_grads = lax.scan(
        one_block,
        (empty, empty),
        (query_blocks, grad_blocks, log_total, jnp.arange(seq_count * block_count)),
    )
    return (
        query_grads.reshape(query_rows.shape[0], -1),
        key_grads.reshape(key_rows.shape[0], -1),
        value_grads.reshape(key_rows.shape[0], -1),
    )


def spread(left_side, weight):

    def partial_term(first_row, row_count):
        return product(left_side, weight)

    return lax.psum_scatter(
        partial_term(
            jnp.int32(0), left_side.shape[0] // lax.axis_size("col") * lax.axis_size("col")
        ),
        "col",
        scatter_dimension=0,
        tiled=True,
    )


def spread_back(grad_pairs):

    def partial_term(first_row, row_count):
        summed = against(grad_pairs[0][0], grad_pairs[0][1])
        for gradient, weight in grad_pairs[1:]:
            summed = summed + against(gradient, weight)
        return summed

    return lax.psum_scatter(
        partial_term(
            jnp.int32(0), grad_pairs[0][0].shape[0] // lax.axis_size("col") * lax.axis_size("col")
        ),
        "col",
        scatter_dimension=0,
        tiled=True,
    )


def collect_rows(values):
    return lax.all_gather(values, "col", axis=0, tiled=True)


def collect_grads(values):
    return lax.all_gather(values, "col", axis=0, tiled=True)


def fetch_blocks(
    self_query,
    self_key,
    self_value,
    self_output,
    cross_query,
    cross_key,
    cross_value,
    cross_output,
    expand,
    contract,
):
    return (
        lax.all_gather(self_query, "row", axis=0, tiled=True),
        lax.all_gather(self_key, "row", axis=0, tiled=True),
        lax.all_gather(self_value, "row", axis=0, tiled=True),
        lax.all_gather(self_output, "row", axis=1, tiled=True),
        lax.all_gather(cross_query, "row", axis=0, tiled=True),
        lax.all_gather(cross_key, "row", axis=0, tiled=True),
        lax.all_gather(cross_value, "row", axis=0, tiled=True),
        lax.all_gather(cross_output, "row", axis=1, tiled=True),
        lax.all_gather(expand, "row", axis=0, tiled=True),
        lax.all_gather(contract, "row", axis=1, tiled=True),
    )


def per_device(
    tokens,
    encoded,
    source_len,
    out_grad,
    self_query,
    self_key,
    self_value,
    self_output,
    self_query_bias,
    self_value_bias,
    self_output_bias,
    cross_query,
    cross_key,
    cross_value,
    cross_output,
    cross_query_bias,
    cross_value_bias,
    cross_output_bias,
    expand,
    expand_bias,
    contract,
    contract_bias,
    attn_gain,
    attn_shift,
    cross_gain,
    cross_shift,
    final_gain,
    final_shift,
):
    row_devices = lax.axis_size("row")
    column = lax.axis_index("col")
    head_width = self_query.shape[1]
    hidden_width = expand.shape[1]
    query_scale = HEAD_DIM ** (-0.5)
    local_blocks = (
        self_query,
        self_key,
        self_value,
        self_output,
        cross_query,
        cross_key,
        cross_value,
        cross_output,
        expand,
        contract,
    )
    gathered_dims = (0, 0, 0, 1, 0, 0, 0, 1, 0, 1)
    block_shapes = [
        (
            (block.shape[0] * row_devices, block.shape[1])
            if along == 0
            else (block.shape[0], block.shape[1] * row_devices)
        )
        for block, along in zip(local_blocks, gathered_dims)
    ]

    def piece(vector, part_size):
        return lax.dynamic_slice_in_dim(vector, column * part_size, part_size)

    bias_query = piece(self_query_bias, head_width)
    bias_value = piece(self_value_bias, head_width)
    bias_cquery = piece(cross_query_bias, head_width)
    bias_cvalue = piece(cross_value_bias, head_width)
    bias_hidden = piece(expand_bias, hidden_width)
    totals = [jnp.zeros(shape, jnp.float32) for shape in block_shapes]
    small_shapes = (
        head_width,
        head_width,
        tokens.shape[2],
        head_width,
        head_width,
        tokens.shape[2],
        hidden_width,
        tokens.shape[2],
        tokens.shape[2],
        tokens.shape[2],
        tokens.shape[2],
        tokens.shape[2],
        tokens.shape[2],
        tokens.shape[2],
    )
    small = [jnp.zeros((shape,), jnp.float32) for shape in small_shapes]
    result_list = []
    tokens_list = []
    encoded_list = []
    micro_count = tokens.shape[0]
    for micro_step in range(micro_count):
        blocks_now = fetch_blocks(
            self_query,
            self_key,
            self_value,
            self_output,
            cross_query,
            cross_key,
            cross_value,
            cross_output,
            expand,
            contract,
        )
        (
            w_query,
            w_key,
            w_value,
            w_output,
            w_cquery,
            w_ckey,
            w_cvalue,
            w_coutput,
            w_expand,
            w_contract,
        ) = blocks_now
        token_rows, encoder_rows = (
            lax.all_gather(tokens[micro_step], "col", axis=0, tiled=True),
            lax.all_gather(encoded[micro_step], "col", axis=0, tiled=True),
        )
        source_now = source_len[micro_step]
        seq_count = source_now.shape[0]
        cross_allowed = source_rule(source_now)
        query_rows = ((product(token_rows, w_query) + bias_query) * query_scale).astype(
            jnp.bfloat16
        )
        key_rows = product(token_rows, w_key).astype(jnp.bfloat16)
        value_rows = (product(token_rows, w_value) + bias_value).astype(jnp.bfloat16)
        mixed_heads, self_stats = attend(query_rows, key_rows, value_rows, seq_count, causal_rule)
        branch_out = spread(mixed_heads, w_output)
        first_out, first_normed, first_inverse = norm_forward(
            tokens[micro_step].astype(jnp.float32) + branch_out + self_output_bias,
            attn_gain,
            attn_shift,
        )
        first_rows = collect_rows(first_out.astype(jnp.bfloat16))
        cross_rows = ((product(first_rows, w_cquery) + bias_cquery) * query_scale).astype(
            jnp.bfloat16
        )
        cross_keys = product(encoder_rows, w_ckey).astype(jnp.bfloat16)
        cross_values = (product(encoder_rows, w_cvalue) + bias_cvalue).astype(jnp.bfloat16)
        cross_mixed, cross_stats = attend(
            cross_rows, cross_keys, cross_values, seq_count, cross_allowed
        )
        branch_out = spread(cross_mixed, w_coutput)
        second_out, second_normed, second_inverse = norm_forward(
            first_out + branch_out + cross_output_bias, cross_gain, cross_shift
        )
        second_rows = collect_rows(second_out.astype(jnp.bfloat16))
        inner_act = product(second_rows, w_expand) + bias_hidden
        hidden = jax.nn.silu(inner_act).astype(jnp.bfloat16)
        branch_out = spread(hidden, w_contract)
        result_now, third_normed, third_inverse = norm_forward(
            second_out + branch_out + contract_bias, final_gain, final_shift
        )
        result_list.append(result_now)
        blocks_now = fetch_blocks(
            self_query,
            self_key,
            self_value,
            self_output,
            cross_query,
            cross_key,
            cross_value,
            cross_output,
            expand,
            contract,
        )
        (
            w_query,
            w_key,
            w_value,
            w_output,
            w_cquery,
            w_ckey,
            w_cvalue,
            w_coutput,
            w_expand,
            w_contract,
        ) = blocks_now
        gradient, final_gain_part, final_shift_part = norm_backward(
            out_grad[micro_step], third_normed, third_inverse, final_gain
        )
        contract_bias_part = jnp.sum(gradient, axis=0)
        grad_rows = collect_grads(gradient.astype(jnp.bfloat16))
        contract_part = over_rows(hidden, grad_rows)
        hidden_back = against(grad_rows, w_contract)
        logistic = jax.nn.sigmoid(inner_act)
        inner_back = (hidden_back * logistic * (1.0 + inner_act * (1.0 - logistic))).astype(
            jnp.bfloat16
        )
        expand_bias_part = jnp.sum(inner_back.astype(jnp.float32), axis=0)
        expand_part = over_rows(second_rows, inner_back)
        back_rows = spread_back(((inner_back, w_expand),))
        gradient, cross_gain_part, cross_shift_part = norm_backward(
            gradient + back_rows, second_normed, second_inverse, cross_gain
        )
        cross_output_bias_part = jnp.sum(gradient, axis=0)
        grad_rows = collect_grads(gradient.astype(jnp.bfloat16))
        coutput_part = over_rows(cross_mixed, grad_rows)
        cross_mixed_back = against(grad_rows, w_coutput).astype(jnp.bfloat16)
        cross_rows_back, cross_keys_back, cross_values_back = attend_back(
            cross_rows,
            cross_keys,
            cross_values,
            cross_stats,
            cross_mixed_back,
            seq_count,
            cross_allowed,
        )
        cross_rows_back = cross_rows_back.astype(jnp.bfloat16) * query_scale
        cross_keys_back = cross_keys_back.astype(jnp.bfloat16)
        cross_values_back = cross_values_back.astype(jnp.bfloat16)
        cquery_bias_part = jnp.sum(cross_rows_back.astype(jnp.float32), axis=0)
        cvalue_bias_part = jnp.sum(cross_values_back.astype(jnp.float32), axis=0)
        cquery_part = over_rows(first_rows, cross_rows_back)
        ckey_part = over_rows(encoder_rows, cross_keys_back)
        cvalue_part = over_rows(encoder_rows, cross_values_back)
        back_first, back_encoder = (
            lax.psum_scatter(
                against(cross_rows_back, w_cquery).astype(jnp.bfloat16),
                "col",
                scatter_dimension=0,
                tiled=True,
            ).astype(jnp.float32),
            lax.psum_scatter(
                (against(cross_keys_back, w_ckey) + against(cross_values_back, w_cvalue)).astype(
                    jnp.bfloat16
                ),
                "col",
                scatter_dimension=0,
                tiled=True,
            ).astype(jnp.float32),
        )
        encoded_list.append(back_encoder)
        gradient, attn_gain_part, attn_shift_part = norm_backward(
            gradient + back_first, first_normed, first_inverse, attn_gain
        )
        self_output_bias_part = jnp.sum(gradient, axis=0)
        grad_rows = collect_grads(gradient.astype(jnp.bfloat16))
        output_part = over_rows(mixed_heads, grad_rows)
        mixed_back = against(grad_rows, w_output).astype(jnp.bfloat16)
        query_back, key_back, value_back = attend_back(
            query_rows, key_rows, value_rows, self_stats, mixed_back, seq_count, causal_rule
        )
        query_back = query_back.astype(jnp.bfloat16) * query_scale
        key_back = key_back.astype(jnp.bfloat16)
        value_back = value_back.astype(jnp.bfloat16)
        query_bias_part = jnp.sum(query_back.astype(jnp.float32), axis=0)
        value_bias_part = jnp.sum(value_back.astype(jnp.float32), axis=0)
        query_part = over_rows(token_rows, query_back)
        key_part = over_rows(token_rows, key_back)
        value_part = over_rows(token_rows, value_back)
        back_rows = spread_back(((query_back, w_query), (key_back, w_key), (value_back, w_value)))
        tokens_list.append(gradient + back_rows)
        section_grads = (
            query_part,
            key_part,
            value_part,
            output_part,
            cquery_part,
            ckey_part,
            cvalue_part,
            coutput_part,
            expand_part,
            contract_part,
        )
        totals = [running + fresh for running, fresh in zip(totals, section_grads)]
        section_small = (
            query_bias_part,
            value_bias_part,
            self_output_bias_part,
            cquery_bias_part,
            cvalue_bias_part,
            cross_output_bias_part,
            expand_bias_part,
            contract_bias_part,
            attn_gain_part,
            attn_shift_part,
            cross_gain_part,
            cross_shift_part,
            final_gain_part,
            final_shift_part,
        )
        small = [running + fresh for running, fresh in zip(small, section_small)]
    totals = (
        *sent_together(
            (
                totals[0].astype(jnp.bfloat16),
                totals[1].astype(jnp.bfloat16),
                totals[2].astype(jnp.bfloat16),
            ),
            "row",
            0,
            1,
        ),
        summed_on_arrival(totals[3].astype(jnp.bfloat16), "row", 1),
        *sent_together(
            (
                totals[4].astype(jnp.bfloat16),
                totals[5].astype(jnp.bfloat16),
                totals[6].astype(jnp.bfloat16),
            ),
            "row",
            0,
            1,
        ),
        summed_on_arrival(totals[7].astype(jnp.bfloat16), "row", 1),
        summed_on_arrival(totals[8].astype(jnp.bfloat16), "row", 0),
        summed_on_arrival(totals[9].astype(jnp.bfloat16), "row", 1),
    )
    model_width = tokens.shape[2]
    full_hidden = hidden_width * lax.axis_size("col")

    def place(part_vec, whole):
        return lax.dynamic_update_slice_in_dim(
            jnp.zeros((whole,), jnp.float32), part_vec, column * part_vec.shape[0], 0
        )

    reduced_small = lax.psum(
        (
            place(small[0], model_width),
            place(small[1], model_width),
            small[2],
            place(small[3], model_width),
            place(small[4], model_width),
            small[5],
            place(small[6], full_hidden),
            small[7],
            small[8],
            small[9],
            small[10],
            small[11],
            small[12],
            small[13],
        ),
        ("row", "col"),
    )
    return (
        jnp.stack(result_list),
        jnp.stack(tokens_list),
        jnp.stack(encoded_list),
        totals[0],
        totals[1],
        totals[2],
        totals[3],
        reduced_small[0],
        reduced_small[1],
        reduced_small[2],
        totals[4],
        totals[5],
        totals[6],
        totals[7],
        reduced_small[3],
        reduced_small[4],
        reduced_small[5],
        totals[8],
        reduced_small[6],
        totals[9],
        reduced_small[7],
        reduced_small[8],
        reduced_small[9],
        reduced_small[10],
        reduced_small[11],
        reduced_small[12],
        reduced_small[13],
    )


def solution(mesh):
    return jax.shard_map(
        per_device,
        mesh=mesh,
        in_specs=(
            P(None, ("row", "col"), None),
            P(None, ("row", "col"), None),
            P(None, "row"),
            P(None, ("row", "col"), None),
            P("row", "col"),
            P("row", "col"),
            P("row", "col"),
            P("col", "row"),
            P(),
            P(),
            P(),
            P("row", "col"),
            P("row", "col"),
            P("row", "col"),
            P("col", "row"),
            P(),
            P(),
            P(),
            P("row", "col"),
            P(),
            P("col", "row"),
            P(),
            P(),
            P(),
            P(),
            P(),
            P(),
            P(),
        ),
        out_specs=(
            P(None, ("row", "col"), None),
            P(None, ("row", "col"), None),
            P(None, ("row", "col"), None),
            P("row", "col"),
            P("row", "col"),
            P("row", "col"),
            P("col", "row"),
            P(),
            P(),
            P(),
            P("row", "col"),
            P("row", "col"),
            P("row", "col"),
            P("col", "row"),
            P(),
            P(),
            P(),
            P("row", "col"),
            P(),
            P("col", "row"),
            P(),
            P(),
            P(),
            P(),
            P(),
            P(),
            P(),
        ),
        check_vma=False,
    )
```

profile of v0, /device:TPU:0, one launch (start us, length us, event | category | flops | bytes accessed | tf_op | source)
XLA Modules:
  0.0 1050.3 jit_solution(4809110193620711342)
XLA Ops:
  9.9 10.9 %all_gather.49 = bf16[512,128]{1,0:T(8,128)(2,1)S(1)} all-gather(bf16[64,128]{1,0:T(8,128)(2,1)} %param.64), channel_id=1, replica_groups=mesh['row'=8,'col'=4] {'row'}, dimensions={0}, use_global_device_ids=true | all-gather | bytes 147456 | tf_op jit(solution)/shard_map/all_gather | solution.py:225
  22.3 9.0 all_gather.51
  31.3 8.4 all_gather.50
  39.7 9.0 all_gather.52
  53.4 12.9 %while.132 = (s32[]{:T(128)}, bf16[2,512,2,64]{1,3,2,0:T(8,128)(2,1)S(1)}, f32[2,2,512]{2,1,0:T(2,128)S(1)}, s32[2]{0:T(128)S(1)}, bf16[2,512,2,64]{1,3,2,0:T(8,...) while((s32[]{:T(128)}, ...), condition=%wide.region_20.21_spmd, body=%wide.region_17.20_spmd.sunk | while | flops 278461952 | bytes 15503618 | solution.py:111
  75.7 14.1 %while.130 = (s32[]{:T(128)}, bf16[2,512,2,64]{1,3,2,0:T(8,128)(2,1)S(1)}, f32[2,2,512]{2,1,0:T(2,128)}, s32[2]{0:T(128)S(1)}, bf16[2,512,2,64]{1,3,2,0:T(8,128)...) while((s32[]{:T(128)}, ...), condition=%wide.region_3.4_spmd, body=%wide.region_0.3_spmd.sunk | while | flops 278461952 | bytes 15504126 | solution.py:111
  93.6 22.2 %reduce-scatter.21.cloned.1.call-done = f32[256,512]{1,0:T(8,128)} async-done(((f32[1024,512]{1,0:T(8,128)}), f32[256,512]{1,0:T(8,128)}) %reduce-scatter.21.cloned.1.call-update) | async-done | bytes 524304 | tf_op jit(solution)/shard_map/reduce_scatter | solution.py:176
  115.8 45.0 %reduce-scatter.15.cloned.1.call-done = f32[256,512]{1,0:T(8,128)} async-done(((f32[1024,512]{1,0:T(8,128)}), f32[256,512]{1,0:T(8,128)}) %reduce-scatter.15.cloned.1.call-update) | async-done | bytes 524304 | tf_op jit(solution)/shard_map/reduce_scatter | solution.py:176
  165.2 9.2 all_gather.108
  174.4 9.1 all_gather.111
  183.6 8.2 all_gather.110
  191.8 9.1 all_gather.112
  205.7 12.5 %all-gather.41.cloned.1.call-done = bf16[1,1024,512]{2,1,0:T(8,128)(2,1)} async-done(((bf16[1,256,512]{2,1,0:T(8,128)(2,1)}), bf16[1,1024,512]{2,1,0:T(8,128)(2,1)}) %all-gather.41.cloned.1.call-update) | async-done | bytes 1048592 | tf_op jit(solution)/shard_map/all_gather | solution.py:352
  221.1 26.6 %all-gather.23.cloned.1.call-done = bf16[1024,512]{1,0:T(8,128)(2,1)} async-done(((bf16[256,512]{1,0:T(8,128)(2,1)}), bf16[1024,512]{1,0:T(8,128)(2,1)}) %all-gather.23.cloned.1.call-update) | async-done | bytes 1048592 | tf_op jit(solution)/shard_map/all_gather | solution.py:205
  250.1 9.2 while.133
  263.2 14.1 %all-gather.19.cloned.1.call-done = bf16[1024,512]{1,0:T(8,128)(2,1)} async-done(((bf16[256,512]{1,0:T(8,128)(2,1)}), bf16[1024,512]{1,0:T(8,128)(2,1)}) %all-gather.19.cloned.1.call-update) | async-done | bytes 1048592 | tf_op jit(solution)/shard_map/all_gather | solution.py:205
  280.3 10.3 while.131
  292.9 29.8 %reduce-scatter.23.cloned.1.call-done = f32[256,512]{1,0:T(8,128)} async-done(((f32[1024,512]{1,0:T(8,128)}), f32[256,512]{1,0:T(8,128)}) %reduce-scatter.23.cloned.1.call-update) | async-done | bytes 524304 | tf_op jit(solution)/shard_map/reduce_scatter | solution.py:176
  322.7 45.2 %reduce-scatter.17.cloned.1.call-done = f32[256,512]{1,0:T(8,128)} async-done(((f32[1024,512]{1,0:T(8,128)}), f32[256,512]{1,0:T(8,128)}) %reduce-scatter.17.cloned.1.call-update) | async-done | bytes 524304 | tf_op jit(solution)/shard_map/reduce_scatter | solution.py:176
  372.4 9.8 all_gather.114
  382.2 9.8 all_gather.115
  392.0 6.4 all-gather.21.cloned.1.call-done
  405.1 22.6 %all-gather.25.cloned.1.call-done = bf16[1024,512]{1,0:T(8,128)(2,1)} async-done(((bf16[256,512]{1,0:T(8,128)(2,1)}), bf16[1024,512]{1,0:T(8,128)(2,1)}) %all-gather.25.cloned.1.call-update) | async-done | bytes 1048592 | tf_op jit(solution)/shard_map/all_gather | solution.py:205
  433.3 39.8 %reduce-scatter.19.cloned.1.call-done = f32[256,512]{1,0:T(8,128)} async-done(((f32[1024,512]{1,0:T(8,128)}), f32[256,512]{1,0:T(8,128)}) %reduce-scatter.19.cloned.1.call-update) | async-done | bytes 524304 | tf_op jit(solution)/shard_map/reduce_scatter | solution.py:176
  473.1 45.0 %reduce-scatter.25.cloned.1.call-done = f32[256,512]{1,0:T(8,128)} async-done(((f32[1024,512]{1,0:T(8,128)}), f32[256,512]{1,0:T(8,128)}) %reduce-scatter.25.cloned.1.call-update) | async-done | bytes 524304 | tf_op jit(solution)/shard_map/reduce_scatter | solution.py:176
  529.4 25.4 %all-gather.27.cloned.1.call-done = bf16[1024,512]{1,0:T(8,128)(2,1)} async-done(((bf16[256,512]{1,0:T(8,128)(2,1)}), bf16[1024,512]{1,0:T(8,128)(2,1)}) %all-gather.27.cloned.1.call-update) | async-done | bytes 1048592 | tf_op jit(solution)/shard_map/all_gather | solution.py:209
  554.8 3.9 convert_reduce_fusion.1
  561.9 21.7 %all-gather.33.cloned.1.call-done = bf16[1024,512]{1,0:T(8,128)(2,1)} async-done(((bf16[256,512]{1,0:T(8,128)(2,1)}), bf16[1024,512]{1,0:T(8,128)(2,1)}) %all-gather.33.cloned.1.call-update) | async-done | bytes 1048592 | tf_op jit(solution)/shard_map/all_gather | solution.py:209
  583.6 3.8 convert_reduce_fusion
  590.5 38.3 %reduce-scatter.27.cloned.1.call-done = f32[256,512]{1,0:T(8,128)} async-done(((f32[1024,512]{1,0:T(8,128)}), f32[256,512]{1,0:T(8,128)}) %reduce-scatter.27.cloned.1.call-update) | async-done | bytes 524304 | tf_op jit(solution)/shard_map/reduce_scatter | solution.py:194
  630.9 42.9 %reduce-scatter.33.cloned.1.call-done = f32[256,512]{1,0:T(8,128)} async-done(((f32[1024,512]{1,0:T(8,128)}), f32[256,512]{1,0:T(8,128)}) %reduce-scatter.33.cloned.1.call-update) | async-done | bytes 524304 | tf_op jit(solution)/shard_map/reduce_scatter | solution.py:194
  679.4 24.8 %all-gather.29.cloned.1.call-done = bf16[1024,512]{1,0:T(8,128)(2,1)} async-done(((bf16[256,512]{1,0:T(8,128)(2,1)}), bf16[1024,512]{1,0:T(8,128)(2,1)}) %all-gather.29.cloned.1.call-update) | async-done | bytes 1048592 | tf_op jit(solution)/shard_map/all_gather | solution.py:209
  707.7 32.2 %while.134 = (s32[]{:T(128)}, f32[1,1024,2,64]{1,3,2,0:T(8,128)}, f32[1,1024,2,64]{1,3,2,0:T(8,128)}, bf16[2,512,2,64]{1,3,2,0:T(8,128)(2,1)}, s32[2]{0:T(128)},...) while((s32[]{:T(128)}, f32[1,1024,2,64]{1,3,2,0:T(8,128)}, ...), condition=%wide.region_42.43_spmd.clone, body=%wide.region_39.42_spmd.clone.sunk | while | flops 684457984 | bytes 68715496 | solution.py:159
  747.2 29.4 %while.136 = (s32[]{:T(128)}, f32[1,1024,2,64]{1,3,2,0:T(8,128)S(1)}, f32[1,1024,2,64]{1,3,2,0:T(8,128)}, bf16[2,512,2,64]{1,3,2,0:T(8,128)(2,1)}, s32[2]{0:T(12...) while((s32[]{:T(128)}, ...), condition=%wide.region_59.60_spmd.clone, body=%wide.region_56.59_spmd.clone.sunk | while | flops 684457984 | bytes 68715496 | solution.py:159
  783.2 24.6 %reduce-scatter.35.cloned.1.call-done = bf16[256,512]{1,0:T(8,128)(2,1)} async-done(((bf16[1024,512]{1,0:T(8,128)(2,1)}), bf16[256,512]{1,0:T(8,128)(2,1)}) %reduce-scatter.35.cloned.1.call-update) | async-done | bytes 262160 | tf_op jit(solution)/shard_map/reduce_scatter | solution.py:453
  820.5 3.7 fusion.193
  824.2 4.3 all-to-all-start.5
  855.3 33.4 %while.135 = (s32[]{:T(128)}, f32[1,1024,2,64]{1,3,2,0:T(8,128)}, f32[1,1024,2,64]{1,3,2,0:T(8,128)}, bf16[2,512,2,64]{1,3,2,0:T(8,128)(2,1)}, s32[2]{0:T(128)S(...) while((s32[]{:T(128)}, f32[1,1024,2,64]{1,3,2,0:T(8,128)}, ...), condition=%wide.region_49.50_spmd.clone, body=%wide.region_46.49_spmd.clone.sunk | while | flops 684981760 | bytes 72910880 | solution.py:159
  867.5 3.7 fusion.495
  884.7 3.9 fusion.495
  899.2 34.0 %while.137 = (s32[]{:T(128)}, f32[1,1024,2,64]{1,3,2,0:T(8,128)}, f32[1,1024,2,64]{1,3,2,0:T(8,128)}, bf16[2,512,2,64]{1,3,2,0:T(8,128)(2,1)}, s32[2]{0:T(128)},...) while((s32[]{:T(128)}, f32[1,1024,2,64]{1,3,2,0:T(8,128)}, ...), condition=%wide.region_66.67_spmd.clone, body=%wide.region_63.66_spmd.clone.sunk | while | flops 684981760 | bytes 72910880 | solution.py:159
  911.9 3.7 fusion.519
  929.3 3.9 fusion.519
  942.0 4.2 all-to-all-start.4
  946.2 3.6 add_add_fusion
  951.3 4.6 all-to-all-done.4
  990.0 3.7 all-to-all-start
  998.0 40.7 %all-reduce = (f32[512]{0:T(512)}, f32[512]{0:T(512)}, f32[512]{0:T(512)}, f32[512]{0:T(512)}, f32[512]{0:T(512)}, /*index=5*/f32[512]{0:T(512)}, f32[2048]{0:T(...) all-reduce(f32[512]{0:T(512)S(1)} %dynamic_update_slice.82, ...), channel_id=1, replica_groups=mesh['row'=8,'col'=4] {'row','col'}, use_global_device_ids=true, to_apply=%region_74.75 | all-reduce | flops 8704 | bytes 69632 | tf_op jit(solution)/shard_map/psum | solution.py:553
  (792 shorter events, 337.2 us)
Async XLA Ops:
  7.2 41.5 %all-gather.43.cloned.1.call-start = ((), (), s32[]{:S(2)}) async-start(), calls=%async_computation.46 | async-start | bytes 1310720 | tf_op jit(solution)/shard_map/all_gather | solution.py:351
  9.1 61.3 %all-gather.39.cloned.1.call-start = ((), (), s32[]{:S(2)}) async-start(), calls=%async_computation.44 | async-start | bytes 1310720 | tf_op jit(solution)/shard_map/all_gather | solution.py:351
  9.9 105.9 %reduce-scatter.21.cloned.1.call-start = ((), (), s32[]{:S(2)}) async-start(), calls=%async_computation.25 | async-start | bytes 2621440 | tf_op jit(solution)/shard_map/reduce_scatter | solution.py:176
  68.6 92.2 %reduce-scatter.15.cloned.1.call-start = ((), (), s32[]{:S(2)}) async-start(), calls=%async_computation.20 | async-start | bytes 2621440 | tf_op jit(solution)/shard_map/reduce_scatter | solution.py:176
  92.0 82.4 %copy-start.117 = (bf16[64,128]{1,0:T(8,128)(2,1)S(1)}, bf16[64,128]{1,0:T(8,128)(2,1)}, u32[]{:S(2)}) copy-start(bf16[64,128]{1,0:T(8,128)(2,1)} %param.73) | copy-start | bytes 49156
  92.0 91.5 %copy-start.118 = (bf16[64,128]{1,0:T(8,128)(2,1)S(1)}, bf16[64,128]{1,0:T(8,128)(2,1)}, u32[]{:S(2)}) copy-start(bf16[64,128]{1,0:T(8,128)(2,1)} %param.72) | copy-start | bytes 49156
  92.0 99.8 %copy-start.119 = (bf16[128,64]{0,1:T(8,128)(2,1)S(1)}, bf16[128,64]{0,1:T(8,128)(2,1)}, u32[]{:S(2)}) copy-start(bf16[128,64]{0,1:T(8,128)(2,1)} %param.74) | copy-start | bytes 49156
  92.0 108.9 %copy-start.164 = (s32[2,1]{0,1:T(1,128)S(1)}, s32[2,1]{0,1:T(1,128)}, u32[]{:S(2)}) copy-start(s32[2,1]{0,1:T(1,128)} %param.62) | copy-start | bytes 28
  92.1 109.5 %all-gather.45.cloned.1.call-start = ((), (), s32[]{:S(2)}) async-start(), calls=%async_computation.47 | async-start | bytes 1310720 | tf_op jit(solution)/shard_map/all_gather | solution.py:352
  93.0 125.2 %all-gather.41.cloned.1.call-start = ((), (), s32[]{:S(2)}) async-start(), calls=%async_computation.45 | async-start | bytes 1310720 | tf_op jit(solution)/shard_map/all_gather | solution.py:352
  93.5 154.2 %all-gather.23.cloned.1.call-start = ((), (), s32[]{:S(2)}) async-start(), calls=%async_computation.26 | async-start | bytes 1310720 | tf_op jit(solution)/shard_map/all_gather | solution.py:205
  162.2 205.6 %copy-start.23 = (f32[256,512]{1,0:T(8,128)}, f32[256,512]{1,0:T(8,128)S(1)}, u32[]{:S(2)}) copy-start(f32[256,512]{1,0:T(8,128)S(1)} %get-tuple-element.1472) | copy-start | bytes 1572868
  162.2 205.6 %copy-start.25 = (f32[256,512]{1,0:T(8,128)}, f32[256,512]{1,0:T(8,128)S(1)}, u32[]{:S(2)}) copy-start(f32[256,512]{1,0:T(8,128)S(1)} %get-tuple-element.1500) | copy-start | bytes 1572868
  163.6 113.7 %all-gather.19.cloned.1.call-start = ((), (), s32[]{:S(2)}) async-start(), calls=%async_computation.21 | async-start | bytes 1310720 | tf_op jit(solution)/shard_map/all_gather | solution.py:205
  174.4 102.9 %copy-start.88 = (bf16[512,128]{1,0:T(8,128)(2,1)}, bf16[512,128]{1,0:T(8,128)(2,1)S(1)}, u32[]{:S(2)}) copy-start(bf16[512,128]{1,0:T(8,128)(2,1)S(1)} %all_gather.108) | copy-start | bytes 393220
  220.7 102.0 %reduce-scatter.23.cloned.1.call-start = ((), (), s32[]{:S(2)}) async-start(), calls=%async_computation.27 | async-start | bytes 2621440 | tf_op jit(solution)/shard_map/reduce_scatter | solution.py:176
  261.4 106.4 %reduce-scatter.17.cloned.1.call-start = ((), (), s32[]{:S(2)}) async-start(), calls=%async_computation.22 | async-start | bytes 2621440 | tf_op jit(solution)/shard_map/reduce_scatter | solution.py:176
  292.8 79.6 %copy-start.100 = (bf16[64,512]{1,0:T(8,128)(2,1)S(1)}, bf16[64,512]{1,0:T(8,128)(2,1)}, u32[]{:S(2)}) copy-start(bf16[64,512]{1,0:T(8,128)(2,1)} %param.78) | copy-start | bytes 196612
  292.8 89.4 %copy-start.101 = (bf16[512,64]{0,1:T(8,128)(2,1)S(1)}, bf16[512,64]{0,1:T(8,128)(2,1)}, u32[]{:S(2)}) copy-start(bf16[512,64]{0,1:T(8,128)(2,1)} %param.80) | copy-start | bytes 196612
  292.8 105.6 %all-gather.21.cloned.1.call-start = ((), (), s32[]{:S(2)}) async-start(), calls=%async_computation.23 | async-start | bytes 1310720 | tf_op jit(solution)/shard_map/all_gather | solution.py:205
  371.0 56.7 %all-gather.25.cloned.1.call-start = ((), (), s32[]{:S(2)}) async-start(), calls=%async_computation.28 | async-start | bytes 1310720 | tf_op jit(solution)/shard_map/all_gather | solution.py:205
  371.6 101.5 %reduce-scatter.19.cloned.1.call-start = ((), (), s32[]{:S(2)}) async-start(), calls=%async_computation.24 | async-start | bytes 2621440 | tf_op jit(solution)/shard_map/reduce_scatter | solution.py:176
  372.4 211.2 %copy-start.160 = (f32[512]{0:T(512)}, f32[512]{0:T(512)S(1)}, u32[]{:S(2)}) copy-start(f32[512]{0:T(512)S(1)} %dynamic_slice.174) | copy-start | bytes 6148
  404.9 113.2 %reduce-scatter.25.cloned.1.call-start = ((), (), s32[]{:S(2)}) async-start(), calls=%async_computation.29 | async-start | bytes 2621440 | tf_op jit(solution)/shard_map/reduce_scatter | solution.py:176
  431.1 87.0 %copy-start.158 = (f32[512]{0:T(512)S(1)}, f32[512]{0:T(512)}, u32[]{:S(2)}) copy-start(f32[512]{0:T(512)} %param.81) | copy-start | bytes 6148
  433.2 86.9 %copy-start.123 = (f32[512]{0:T(512)S(1)}, f32[512]{0:T(512)}, u32[]{:S(2)}) copy-start(f32[512]{0:T(512)} %param.86) | copy-start | bytes 6148
  433.2 89.3 %copy-start.159 = (f32[512]{0:T(512)S(1)}, f32[512]{0:T(512)}, u32[]{:S(2)}) copy-start(f32[512]{0:T(512)} %param.87) | copy-start | bytes 6148
  433.3 121.5 %all-gather.27.cloned.1.call-start = ((), (), s32[]{:S(2)}) async-start(), calls=%async_computation.30 | async-start | bytes 1310720 | tf_op jit(solution)/shard_map/all_gather | solution.py:209
  527.5 56.1 %all-gather.33.cloned.1.call-start = ((), (), s32[]{:S(2)}) async-start(), calls=%async_computation.36 | async-start | bytes 1310720 | tf_op jit(solution)/shard_map/all_gather | solution.py:209
  529.3 99.5 %reduce-scatter.27.cloned.1.call-start = ((), (), s32[]{:S(2)}) async-start(), calls=%async_computation.31 | async-start | bytes 2621440 | tf_op jit(solution)/shard_map/reduce_scatter | solution.py:194
  561.9 111.9 %reduce-scatter.33.cloned.1.call-start = ((), (), s32[]{:S(2)}) async-start(), calls=%async_computation.37 | async-start | bytes 2621440 | tf_op jit(solution)/shard_map/reduce_scatter | solution.py:194
  587.4 86.4 %copy-start.41 = (f32[256,512]{1,0:T(8,128)S(1)}, f32[256,512]{1,0:T(8,128)}, u32[]{:S(2)}) copy-start(f32[256,512]{1,0:T(8,128)} %get-tuple-element.1496) | copy-start | bytes 1572868
  590.5 113.7 %all-gather.29.cloned.1.call-start = ((), (), s32[]{:S(2)}) async-start(), calls=%async_computation.32 | async-start | bytes 1310720 | tf_op jit(solution)/shard_map/all_gather | solution.py:209
  676.9 65.2 %all-gather.35.cloned.1.call-start = ((), (), s32[]{:S(2)}) async-start(), calls=%async_computation.38 | async-start | bytes 1310720 | tf_op jit(solution)/shard_map/all_gather | solution.py:209
  679.2 102.2 %reduce-scatter.29.cloned.1.call-start = ((), (), s32[]{:S(2)}) async-start(), calls=%async_computation.33 | async-start | bytes 1310720 | tf_op jit(solution)/shard_map/reduce_scatter | solution.py:453
  745.9 61.9 %reduce-scatter.35.cloned.1.call-start = ((), (), s32[]{:S(2)}) async-start(), calls=%async_computation.39 | async-start | bytes 1310720 | tf_op jit(solution)/shard_map/reduce_scatter | solution.py:453
  781.0 71.2 %all-gather.31.cloned.1.call-start = ((), (), s32[]{:S(2)}) async-start(), calls=%async_computation.34 | async-start | bytes 1310720 | tf_op jit(solution)/shard_map/all_gather | solution.py:209
  811.9 76.8 %all-gather.37.cloned.1.call-start = ((), (), s32[]{:S(2)}) async-start(), calls=%async_computation.40 | async-start | bytes 1310720 | tf_op jit(solution)/shard_map/all_gather | solution.py:209
  824.2 117.7 %all-to-all-start.5 = ((bf16[8,512,64]{1,2,0:T(8,128)(2,1)}), bf16[8,512,64]{1,2,0:T(8,128)(2,1)}, u32[]{:S(2)}, u32[]{:S(2)}) async-start(bf16[8,512,64]{1,2,0:T(8,128)(2,1)} %bitcast.73), calls=%async_computation.19 | async-start | bytes 1048576 | tf_op jit(solution)/shard_map/all_to_all | solution.py:21
  828.5 166.7 %reduce-scatter.39.cloned.1.call-start = ((), (), s32[]{:S(2)}) async-start(), calls=%async_computation.42 | async-start | bytes 1310720 | tf_op jit(solution)/shard_map/reduce_scatter | solution.py:459
  831.8 163.5 %reduce-scatter.41.cloned.1.call-start = ((), (), s32[]{:S(2)}) async-start(), calls=%async_computation.43 | async-start | bytes 1310720 | tf_op jit(solution)/shard_map/reduce_scatter | solution.py:459
  844.7 195.3 %reduce-scatter.31.cloned.1.call-start = ((), (), s32[]{:S(2)}) async-start(), calls=%async_computation.35 | async-start | bytes 2621440 | tf_op jit(solution)/shard_map/reduce_scatter | solution.py:194
  942.0 13.9 %all-to-all-start.4 = ((bf16[8,64,512]{2,1,0:T(8,128)(2,1)}), bf16[8,64,512]{2,1,0:T(8,128)(2,1)}, u32[]{:S(2)}, u32[]{:S(2)}) async-start(bf16[8,64,512]{2,1,0:T(8,128)(2,1)} %bitcast.71), calls=%async_computation.18 | async-start | bytes 1048576 | tf_op jit(solution)/shard_map/all_to_all | solution.py:21
  946.1 95.0 %reduce-scatter.37.cloned.1.call-start = ((), (), s32[]{:S(2)}) async-start(), calls=%async_computation.41 | async-start | bytes 2621440 | tf_op jit(solution)/shard_map/reduce_scatter | solution.py:194
  955.9 8.9 all-to-all-start.3
  964.8 11.7 %all-to-all-start.2 = ((bf16[8,64,384]{2,1,0:T(8,128)(2,1)}), bf16[8,64,384]{2,1,0:T(8,128)(2,1)S(1)}, u32[]{:S(2)}, u32[]{:S(2)}) async-start(bf16[8,64,384]{2,1,0:T(8,128)(2,1)} %bitcast.68), calls=%async_computation.16 | async-start | bytes 786432 | tf_op jit(solution)/shard_map/all_to_all | solution.py:21
  981.0 8.9 all-to-all-start.1
  990.0 49.3 %all-to-all-start = ((bf16[8,64,384]{2,1,0:T(8,128)(2,1)}), bf16[8,64,384]{2,1,0:T(8,128)(2,1)S(1)}, u32[]{:S(2)}, u32[]{:S(2)}) async-start(bf16[8,64,384]{2,1,0:T(8,128)(2,1)} %bitcast.63), calls=%async_computation.14 | async-start | bytes 786432 | tf_op jit(solution)/shard_map/all_to_all | solution.py:21
  (167 other events, 2898.2 us)
Sparse Core Ops, SparseCore 0:
  10.2 30.6 all-gather.42
  43.0 27.3 all-gather.38
  72.7 43.0 reduce-scatter.20
  117.9 42.7 reduce-scatter.14
  162.2 27.1 all-gather.44
  190.8 27.3 all-gather.40
  220.3 27.3 all-gather.22
  249.9 27.4 all-gather.18
  279.6 43.0 reduce-scatter.22
  324.8 42.9 reduce-scatter.16
  371.1 27.1 all-gather.20
  400.4 27.3 all-gather.24
  430.0 42.9 reduce-scatter.18
  475.2 42.8 reduce-scatter.24
  527.6 27.1 all-gather.26
  556.2 27.3 all-gather.32
  585.8 42.9 reduce-scatter.26
  630.9 42.8 reduce-scatter.32
  677.0 27.1 all-gather.28
  705.6 27.4 all-gather.34
  746.1 26.6 reduce-scatter.28
  781.1 26.6 reduce-scatter.34
  812.0 26.4 all-gather.30
  839.9 27.4 all-gather.36
  870.3 26.5 reduce-scatter.38
  899.6 25.7 reduce-scatter.40
  927.6 42.1 reduce-scatter.30
  972.0 42.8 reduce-scatter.36
where the time goes:
time: 1060 us; the launch traced here: 1050 us
  waiting for transfers between devices  501 us (47%)
  matrix products  199 us (19%)
  blocking collectives  133 us (13%)
  other arithmetic  97.6 us (9%)
  local copies, waits for them, and re-layouts  47.8 us (5%)
  loops' own time  29.1 us (3%)
  starting transfers between devices  25.5 us (2%)
  between operations  17 us (2%)
    reduce_scatter x6, waiting for transfers between devices, spread(): lax.psum_scatter(partial_term(jnp.int32(0), left_side.shape[0] // lax.axi...  227 us
    reduce_scatter x4, waiting for transfers between devices, spread_back(): lax.psum_scatter(partial_term(jnp.int32(0), grad_pairs[0][0].shape[0] //...  81.2 us
    all_gather x6, waiting for transfers between devices, collect_grads(): return lax.all_gather(values, 'col', axis=0, tiled=True)  72 us
    all_gather x4, waiting for transfers between devices, collect_rows(): return lax.all_gather(values, 'col', axis=0, tiled=True)  69.7 us
    psum x1, blocking collectives, per_device(): lax.psum((place(small[0], model_width), place(small[1], model_width), sma...  40.7 us
    dot_general x20, matrix products, product(): return jnp.dot(left_side, right_side, preferred_element_type=jnp.float32)  36.3 us
    dot_general x20, matrix products, against(): lax.dot_general(left_side, right_side, (((1,), (1,)), ((), ())), preferre...  35 us
    dot_general x20, matrix products, over_rows(): lax.dot_general(left_side, right_side, (((0,), (0,)), ((), ())), preferre...  26.8 us
  transfers between devices with their start and end apart: 34, of which 22 were waited for; matrix products, arithmetic and copies ran while one was open for 29% of the time, Pallas kernels for 0%

commit v1 on v0

v1 whole, which is shorter than its diff:
```python
import functools

import jax
import jax.numpy as jnp
from jax import lax
from jax.experimental import pallas as pl
from jax.experimental.pallas import tpu as pltpu
from jax.sharding import PartitionSpec as P

HEAD_DIM = 64
PAIR = 2 * HEAD_DIM
NEGATIVE = -1e30
EPSILON = 1e-05
ROW, COL = "row", "col"
AXES = (ROW, COL)
MESH = pl.DeviceIdType.MESH
F32 = jnp.float32
BF16 = jnp.bfloat16
VMEM_SPEC = pl.BlockSpec(memory_space=pltpu.VMEM)
SMEM_SPEC = pl.BlockSpec(memory_space=pltpu.SMEM)
ANY_SPEC = pl.BlockSpec(memory_space=pl.ANY)
VMEM_LIMIT = 67_043_328


def dot_nn(a, b):
    return lax.dot_general(a, b, (((1,), (0,)), ((), ())), preferred_element_type=F32)


def dot_nt(a, b):
    return lax.dot_general(a, b, (((1,), (1,)), ((), ())), preferred_element_type=F32)


def dot_tn(a, b):
    return lax.dot_general(a, b, (((0,), (0,)), ((), ())), preferred_element_type=F32)


def norm_forward(values):
    average = jnp.mean(values, axis=1, keepdims=True)
    centered = values - average
    inverse = lax.rsqrt(jnp.mean(centered * centered, axis=1, keepdims=True) + EPSILON)
    return centered * inverse, inverse


def norm_backward(gradient, normed, inverse, gain):
    scaled = gradient * gain
    mean_scaled = jnp.mean(scaled, axis=1, keepdims=True)
    mean_product = jnp.mean(scaled * normed, axis=1, keepdims=True)
    return (scaled - mean_scaled - normed * mean_product) * inverse


def column_sum(values):
    return jnp.sum(values, axis=0, keepdims=True)


def spread_lanes(column, width):
    return jnp.broadcast_to(column, (column.shape[0], width))


def lane_masks():
    lane = lax.broadcasted_iota(jnp.int32, (1, PAIR), 1)
    first = (lane < HEAD_DIM).astype(F32)
    return first, (1.0 - first)


def attend_block(q_ref, kv_ref, out_ref, lse_ref, row0, rows, span, mask):
    first, second = lane_masks()
    halves = (first.astype(BF16), second.astype(BF16))

    def one_pair(z, carry):
        q_pair = q_ref[z, pl.ds(row0, rows), :]
        k_pair = kv_ref[0, z, pl.ds(0, span), :]
        v_pair = kv_ref[1, z, pl.ds(0, span), :]
        outs, stats = [], []
        for half in halves:
            scores = mask(dot_nt(q_pair * half, k_pair))
            row_max = jnp.max(scores, axis=1, keepdims=True)
            raised = jnp.exp(scores - row_max)
            summed = jnp.sum(raised, axis=1, keepdims=True)
            probs = (raised * (1.0 / summed)).astype(BF16)
            outs.append(dot_nn(probs, v_pair))
            stats.append(row_max + jnp.log(summed))
        out_ref[z, pl.ds(row0, rows), :] = (outs[0] * first + outs[1] * second).astype(BF16)
        lse_ref[z, pl.ds(row0, rows), :] = (
            spread_lanes(stats[0], PAIR) * first + spread_lanes(stats[1], PAIR) * second
        )
        return carry

    lax.fori_loop(0, q_ref.shape[0], one_pair, 0)


def attend_block_back(
    q_ref, kv_ref, mixed_ref, lse_ref, grad_ref, dq_ref, dkv_ref, row0, rows, span, chunk, mask
):
    first, second = lane_masks()
    halves = (first.astype(BF16), second.astype(BF16))

    def one_pair(z, carry):
        q_pair = q_ref[z, pl.ds(row0, rows), :]
        g_pair = grad_ref[z, pl.ds(row0, rows), :]
        stats = jnp.transpose(lse_ref[z, pl.ds(row0, rows), :])
        products = jnp.transpose(
            g_pair.astype(F32) * mixed_ref[z, pl.ds(row0, rows), :].astype(F32)
        )
        lse_rows = (stats[0:1, :], stats[HEAD_DIM : HEAD_DIM + 1, :])
        deltas = (column_sum(products[:HEAD_DIM, :]), column_sum(products[HEAD_DIM:, :]))
        q_half = [q_pair * half for half in halves]
        g_half = [g_pair * half for half in halves]
        dq = [jnp.zeros((rows, PAIR), F32), jnp.zeros((rows, PAIR), F32)]
        for at in range(0, span, chunk):
            k_part = kv_ref[0, z, pl.ds(at, chunk), :]
            v_part = kv_ref[1, z, pl.ds(at, chunk), :]
            dk = jnp.zeros((chunk, PAIR), F32)
            dv = jnp.zeros((chunk, PAIR), F32)
            for h in range(2):
                scores = mask(dot_nt(k_part, q_half[h]), at)
                probs = jnp.exp(scores - lse_rows[h])
                prob_grads = dot_nt(v_part, g_half[h])
                score_low = (probs * (prob_grads - deltas[h])).astype(BF16)
                dv = dv + dot_nn(probs.astype(BF16), g_half[h])
                dk = dk + dot_nn(score_low, q_half[h])
                dq[h] = dq[h] + dot_tn(score_low, k_part)
            dkv_ref[0, z, pl.ds(at, chunk), :] += dk
            dkv_ref[1, z, pl.ds(at, chunk), :] += dv
        dq_ref[z, pl.ds(row0, rows), :] = (dq[0] * first + dq[1] * second).astype(
            BF16
        ) * jnp.asarray(HEAD_DIM**-0.5, BF16)
        return carry

    lax.fori_loop(0, q_ref.shape[0], one_pair, 0)


def causal_last(rows, span):
    def mask(scores):
        query = lax.broadcasted_iota(jnp.int32, scores.shape, 0) + (span - rows)
        key = lax.broadcasted_iota(jnp.int32, scores.shape, 1)
        return jnp.where(key <= query, scores, NEGATIVE)

    return mask


def causal_last_back(rows, span):
    def mask(scores, at):
        if at + scores.shape[0] <= span - rows:
            return scores
        key = lax.broadcasted_iota(jnp.int32, scores.shape, 0) + at
        query = lax.broadcasted_iota(jnp.int32, scores.shape, 1) + (span - rows)
        return jnp.where(key <= query, scores, NEGATIVE)

    return mask


class Refs:
    pass


def named(names, refs):
    out = Refs()
    out.__dict__.update(zip(names, refs))
    return out


def flipped(index, bits):
    for bit in bits:
        index = index + bit - 2 * bit * ((index // bit) % 2)
    return index


def bits_of(number):
    return [1 << i for i in range(number.bit_length()) if (number >> i) & 1]


def subsets(bits):
    out = [0]
    for bit in bits:
        out = out + [m + bit for m in out]
    return out


class Links:
    def __init__(self, send, recv):
        self.send, self.recv, self.count, self.open = send, recv, 0, []

    def take(self, amount=1):
        at = self.count
        self.count += amount
        return at

    def copy(self, src, dst, device, send_at, recv_at):
        return pltpu.make_async_remote_copy(
            src_ref=src,
            dst_ref=dst,
            send_sem=self.send.at[send_at],
            recv_sem=self.recv.at[recv_at],
            device_id=device,
            device_id_type=MESH,
        )

    def start(self, src, dst, device):
        at = self.take()
        copy = self.copy(src, dst, device, at, at)
        copy.start()
        self.open.append(copy)
        return copy

    def drain(self):
        for copy in self.open:
            copy.wait_send()
        self.open = []


class Place:
    def __init__(self, row_count, col_count):
        self.rows, self.cols = row_count, col_count
        self.row, self.col = lax.axis_index(ROW), lax.axis_index(COL)
        self.core = self.row % 2
        self.row_bits = bits_of(row_count - 1)
        self.plane_bits = self.row_bits[1:]
        self.half = col_count // 2
        self.members = subsets(self.plane_bits)
        self.sides = ((0, self.plane_bits), (self.half, self.plane_bits[::-1]))
        self.partner = (flipped(self.row, [1]), self.col)
        self.pair_row = (self.row // 2) * 2

    def greet(self):
        barrier = pltpu.get_barrier_semaphore()
        count = 0
        for side in range(2):
            for k in range(self.cols):
                if side + k:
                    device = (
                        flipped(self.row, [1] if side else []),
                        flipped(self.col, bits_of(k)),
                    )
                    pl.semaphore_signal(barrier, inc=1, device_id=device, device_id_type=MESH)
                    count += 1
        for bit in self.plane_bits:
            device = (flipped(self.row, [bit]), self.col)
            pl.semaphore_signal(barrier, inc=1, device_id=device, device_id_type=MESH)
            count += 1
        pl.semaphore_wait(barrier, count)


class Inbound:
    def __init__(self, place, links, source, target):
        self.place, self.links, self.source, self.target = place, links, source, target
        self.part = source.shape[1]
        self.send_at = links.take(2)
        self.recv_at = self.send_at

    def copies(self):
        p = self.place
        slot = p.col // 2
        to_row = p.pair_row + ((p.col + 1) // 2) % 2
        into = self.target.at[pl.ds(pl.multiple_of(slot * self.part, self.part), self.part)]
        out = []
        for b in range(2):
            device = (to_row, 2 * b + p.core)
            out.append(
                self.links.copy(
                    self.source.at[b], into, device, self.send_at + b, self.recv_at + slot
                )
            )
        local = pltpu.make_async_copy(self.source.at[0], into, self.links.recv.at[self.recv_at])
        return out, local

    def stays(self):
        return self.place.col == self.place.core

    def start(self):
        out, local = self.copies()
        out[1].start()

        @pl.when(self.stays())
        def _():
            local.start()

        @pl.when(jnp.logical_not(self.stays()))
        def _():
            out[0].start()

    def arrive(self):
        p = self.place
        for slot in range(2):
            into = self.target.at[pl.ds(slot * self.part, self.part)]
            remote = self.links.copy(
                self.source.at[0], into, p.partner, self.send_at, self.recv_at + slot
            )
            if slot:
                remote.wait_recv()
            else:
                local = pltpu.make_async_copy(
                    self.source.at[0], into, self.links.recv.at[self.recv_at]
                )

                @pl.when(self.stays())
                def _():
                    local.wait()

                @pl.when(jnp.logical_not(self.stays()))
                def _():
                    remote.wait_recv()

    def drain(self):
        out, _ = self.copies()
        out[1].wait_send()

        @pl.when(jnp.logical_not(self.stays()))
        def _():
            out[0].wait_send()


class Outbound:
    def __init__(self, place, links, source, target):
        self.place, self.links, self.source, self.target = place, links, source, target
        self.part = target.shape[1]
        self.send_at = links.take(2)
        self.recv_at = self.send_at

    def copies(self):
        p = self.place
        micro = p.col // 2
        to_row = p.pair_row + p.col % 2
        out = []
        for i, to_col in enumerate((p.core, 3 - p.core)):
            out.append(
                self.links.copy(
                    self.source.at[pl.ds(i * self.part, self.part)],
                    self.target.at[micro],
                    (to_row, to_col),
                    self.send_at + i,
                    self.recv_at + micro,
                )
            )
        local = pltpu.make_async_copy(
            self.source.at[pl.ds(0, self.part)],
            self.target.at[0],
            self.links.recv.at[self.recv_at],
        )
        return out, local

    def stays(self):
        return self.place.col == self.place.core

    def start(self):
        out, local = self.copies()
        out[1].start()

        @pl.when(self.stays())
        def _():
            local.start()

        @pl.when(jnp.logical_not(self.stays()))
        def _():
            out[0].start()

    def arrive(self):
        p = self.place
        for micro in range(2):
            remote = self.links.copy(
                self.source.at[pl.ds(0, self.part)],
                self.target.at[micro],
                p.partner,
                self.send_at,
                self.recv_at + micro,
            )
            if micro:
                remote.wait_recv()
            else:
                _, local = self.copies()

                @pl.when(self.stays())
                def _():
                    local.wait()

                @pl.when(jnp.logical_not(self.stays()))
                def _():
                    remote.wait_recv()

    def drain(self):
        out, _ = self.copies()
        out[1].wait_send()

        @pl.when(jnp.logical_not(self.stays()))
        def _():
            out[0].wait_send()


class Gather:
    def __init__(self, place, links, shard, whole):
        self.place, self.links, self.shard, self.whole = place, links, shard, whole
        self.plane, self.pair = {}, []

    def start(self):
        p = self.place
        self.along = [
            self.links.start(
                self.shard, self.whole.at[p.col, p.row], (p.row, flipped(p.col, bits_of(k)))
            )
            for k in range(1, p.cols)
        ]
        self.whole[p.col, p.row] = self.shard[...]

    def block(self, side, m):
        p = self.place
        return self.whole.at[pl.ds(side, p.half), flipped(p.row, bits_of(m))]

    def send_out(self, side, order, m):
        p = self.place
        reached = max([order.index(b) for b in bits_of(m)], default=-1)
        here = self.block(side, m)
        for bit in order[reached + 1 :]:
            self.plane[(side, m + bit)] = self.links.start(
                here, here, (flipped(p.row, [bit]), p.col)
            )
        self.pair.append(self.links.start(here, here, p.partner))

    def after_col(self):
        for copy in self.along:
            copy.wait_recv()
        for side, order in self.place.sides:
            self.send_out(side, order, 0)

    def after_plane(self, level):
        for side, order in self.place.sides:
            for m in self.place.members:
                if len(bits_of(m)) == level:
                    self.plane[(side, m)].wait_recv()
                    self.send_out(side, order, m)

    def after_planes(self):
        for level in range(1, len(self.place.plane_bits) + 1):
            self.after_plane(level)

    def finish(self):
        for copy in self.pair:
            copy.wait_recv()


class Reduce:
    def __init__(self, place, links, grads, from_pair, from_plane, from_col, out):
        self.place, self.links, self.grads = place, links, grads
        self.sums, self.from_plane, self.from_col, self.out = from_pair, from_plane, from_col, out
        at = 0
        self.bases = []
        for _, order in place.sides:
            bases = []
            for level in range(len(order)):
                bases.append(at)
                at += len(subsets(order[level + 1 :]))
            self.bases.append(bases)

    def start(self):
        p = self.place
        self.pair = [
            self.links.start(
                self.grads.at[:, flipped(p.row, [1] + bits_of(m))], self.sums.at[at], p.partner
            )
            for at, m in enumerate(p.members)
        ]

    def after_pair(self):
        p = self.place
        for at, m in enumerate(p.members):
            self.pair[at].wait_recv()
            own_row = flipped(p.row, bits_of(m))

            def body(i, carry, at=at, own_row=own_row):
                self.sums[at, i] = (
                    self.grads[i, own_row].astype(F32) + self.sums[at, i].astype(F32)
                ).astype(BF16)
                return carry

            lax.fori_loop(0, p.cols, body, 0)
        self.moving = [self.send(side, 0) for side in range(2)]

    def send(self, side_at, level):
        p = self.place
        side, order = p.sides[side_at]
        bit = order[level]
        batch = []
        for slot, m in enumerate(subsets(order[level + 1 :])):
            at = self.bases[side_at][level] + slot
            copy = self.links.start(
                self.sums.at[p.members.index(m + bit), pl.ds(side, p.half)],
                self.from_plane.at[at],
                (flipped(p.row, [bit]), p.col),
            )
            batch.append((m, at, copy))
        return batch

    def after_plane(self, level):
        p = self.place
        last = level + 1 == len(p.plane_bits)
        for side_at in range(2):
            side = p.sides[side_at][0]
            for m, at, copy in self.moving[side_at]:
                copy.wait_recv()
                into = p.members.index(m)

                def body(i, carry, into=into, at=at, side=side):
                    self.sums[into, side + i] = (
                        self.sums[into, side + i].astype(F32)
                        + self.from_plane[at, i].astype(F32)
                    ).astype(BF16)
                    return carry

                lax.fori_loop(0, p.half, body, 0)
            if not last:
                self.moving[side_at] = self.send(side_at, level + 1)
        if last:
            self.along = []
            for k in range(1, p.cols):
                far = flipped(p.col, bits_of(k))
                self.along.append(
                    self.links.start(self.sums.at[0, far], self.from_col.at[k - 1], (p.row, far))
                )

    def finish(self):
        p = self.place
        total = self.sums[0, p.col].astype(F32)
        for k in range(1, p.cols):
            self.along[k - 1].wait_recv()
            total = total + self.from_col[k - 1].astype(F32)
        self.out[...] = total


class Total:
    def __init__(self, place, links, sums, arrived):
        self.place, self.links, self.sums, self.arrived = place, links, sums, arrived
        self.steps = [(b, 0) for b in place.row_bits] + [(b, 1) for b in bits_of(place.cols - 1)]
        self.at = 0

    def start(self):
        p = self.place
        bit, axis = self.steps[self.at]
        device = (flipped(p.row, [bit]), p.col) if axis == 0 else (p.row, flipped(p.col, [bit]))
        self.copy = self.links.start(self.sums.at[self.at % 2], self.arrived.at[self.at], device)

    def step(self):
        if self.at < len(self.steps):
            self.copy.wait_recv()
            if self.at:
                self.before.wait_send()
                self.links.open = [c for c in self.links.open if c is not self.before]
            self.before = self.copy
            at = self.at
            self.sums[(at + 1) % 2] = self.sums[at % 2] + self.arrived[at]
            self.at += 1
            if self.at < len(self.steps):
                self.start()

    def finish(self):
        while self.at < len(self.steps):
            self.step()
        return self.sums[self.at % 2]


def flat_rows(value):
    count, depth, width = value.shape
    if depth % 16 or value.dtype == F32:
        return value.astype(F32).reshape(count * depth, width).astype(value.dtype)
    return value.reshape(count * depth, width)


def row_blocks(value, count):
    return value.reshape(count, value.shape[0] // count, value.shape[1]).astype(BF16)


def layer_kernel(row_count, col_count, names, *refs):
    g = named(names, refs)
    p = Place(row_count, col_count)
    links = Links(g.send, g.recv)
    part = g.tokens.shape[1]
    width = g.tokens.shape[2]
    hid = g.expand.shape[1]
    cols = col_count
    own = 2 * part
    span = 4 * part
    scale = HEAD_DIM**-0.5
    low_at = pl.multiple_of(p.core * part, part)
    high_at = pl.multiple_of((3 - p.core) * part, part)
    other_low = pl.multiple_of((1 - p.core) * part, part)
    other_high = pl.multiple_of((2 + p.core) * part, part)

    def self_w(z, lo=0, hi=3):
        return flat_rows(g.w_self[z, :, :, lo * PAIR : hi * PAIR])

    def attn_w(z, at, count=1):
        return flat_rows(g.w_attn[z, :, :, at * PAIR : (at + count) * PAIR])

    def heads_of(vector, z):
        return vector[:, z * PAIR : (z + 1) * PAIR]

    p.greet()
    x_in = Inbound(p, links, g.tokens, g.x)
    e_in = Inbound(p, links, g.encoded, g.e)
    og_in = Inbound(p, links, g.og_low, g.og)
    x_in.start()
    g.pack_self[:, 0:PAIR] = g.self_query[...]
    g.pack_self[:, PAIR : 2 * PAIR] = g.self_key[...]
    g.pack_self[:, 2 * PAIR :] = g.self_value[...]
    get_self = Gather(p, links, g.pack_self, g.w_self)
    get_self.start()
    for i, shard in enumerate(
        (g.self_output, g.cross_query, g.cross_key, g.cross_value, g.cross_output)
    ):
        value = shard[...]
        if i in (0, 4):
            value = jnp.transpose(value.astype(F32)).astype(BF16)
        g.pack_attn[:, i * PAIR : (i + 1) * PAIR] = value
    get_attn = Gather(p, links, g.pack_attn, g.w_attn)
    g.pack_hidden[:, 0:hid] = g.expand[...]
    g.pack_hidden[:, hid:] = jnp.transpose(g.contract[...].astype(F32)).astype(BF16)
    get_hidden = Gather(p, links, g.pack_hidden, g.w_hidden)
    for m in range(2):
        g.len_own[m] = jnp.full(g.len_own.shape[1:], g.source_len[m, 0], jnp.int32)
    len_copy = links.start(g.len_own, g.len_other, p.partner)
    g.og_low[...] = g.out_grad[...].astype(BF16)
    get_self.after_col()
    get_attn.start()
    e_in.start()
    get_self.after_planes()
    get_attn.after_col()
    get_self.finish()
    x_in.arrive()

    x = g.x[...]
    for z in range(cols):
        rows = dot_nn(x, self_w(z))
        g.q[z] = ((rows[:, 0:PAIR] + heads_of(g.self_query_bias, z)) * scale).astype(BF16)
        k_rows = rows[:, PAIR : 2 * PAIR].astype(BF16)
        v_rows = (rows[:, 2 * PAIR :] + heads_of(g.self_value_bias, z)).astype(BF16)
        for i, value in enumerate((k_rows, v_rows)):
            g.kv[i, z, pl.ds(low_at, part), :] = value[:part]
            g.kv[i, z, pl.ds(high_at, part), :] = value[part:]

    def swap(ref):
        out = []
        for at in (low_at, high_at):
            piece = ref.at[:, :, pl.ds(at, part), :]
            out.append(links.start(piece, piece, p.partner))
        return out

    def swapped(copies):
        for copy in copies:
            copy.wait_recv()

    kv_swap = swap(g.kv)
    get_hidden.start()
    get_attn.after_plane(1)
    swapped(kv_swap)
    for block in range(2):
        for parity in range(2):

            @pl.when(p.core == parity)
            def _():
                keys = (4 - parity if block else parity + 1) * part
                attend_block(
                    g.q, g.kv, g.mixed, g.lse, block * part, part, keys, causal_last(part, keys)
                )

        if block == 0:
            for level in range(2, len(p.plane_bits) + 1):
                get_attn.after_plane(level)
            get_hidden.after_col()
            og_in.start()
    get_attn.finish()
    e_in.arrive()
    len_copy.wait_recv()
    e = g.e[...]
    for z in range(cols):
        rows = dot_nn(e, attn_w(z, 2, 2))
        k_rows = rows[:, :PAIR].astype(BF16)
        v_rows = (rows[:, PAIR:] + heads_of(g.cross_value_bias, z)).astype(BF16)
        for i, value in enumerate((k_rows, v_rows)):
            g.ckv[i, z, pl.ds(low_at, part), :] = value[:part]
            g.ckv[i, z, pl.ds(high_at, part), :] = value[part:]
    ckv_swap = swap(g.ckv)

    branch = g.self_output_bias[...] + g.x[...].astype(F32)
    for z in range(cols):
        branch = branch + dot_nt(g.mixed[z], attn_w(z, 0))
    normed, inverse = norm_forward(branch)
    g.n1[...] = normed
    g.i1[...] = spread_lanes(inverse, PAIR)
    first_low = (normed * g.attn_gain[...] + g.attn_shift[...]).astype(BF16)
    for z in range(cols):
        g.cq[z] = (
            (dot_nn(first_low, attn_w(z, 1)) + heads_of(g.cross_query_bias, z)) * scale
        ).astype(BF16)
    get_hidden.after_plane(1)

    mine = p.col % 2 == p.core
    first_micro = p.col // 2 == 0
    own_len = jnp.where(first_micro, g.len_own[0, 0:1, 0:1], g.len_own[1, 0:1, 0:1])
    other_len = jnp.where(first_micro, g.len_other[0, 0:1, 0:1], g.len_other[1, 0:1, 0:1])
    limit = jnp.where(mine, own_len, other_len)

    def source_mask(scores):
        key = lax.broadcasted_iota(jnp.int32, scores.shape, 1)
        return jnp.where(key < limit, scores, NEGATIVE)

    def source_mask_back(scores, at):
        key = lax.broadcasted_iota(jnp.int32, scores.shape, 0) + at
        return jnp.where(key < limit, scores, NEGATIVE)

    swapped(ckv_swap)
    for block in range(2):
        attend_block(g.cq, g.ckv, g.cmixed, g.clse, block * part, part, span, source_mask)
        if block == 0:
            for level in range(2, len(p.plane_bits) + 1):
                get_hidden.after_plane(level)
    branch = g.n1[...] * g.attn_gain[...] + g.attn_shift[...] + g.cross_output_bias[...]
    for z in range(cols):
        branch = branch + dot_nt(g.cmixed[z], attn_w(z, 4))
    normed, inverse = norm_forward(branch)
    g.n2[...] = normed
    g.i2[...] = spread_lanes(inverse, PAIR)
    get_hidden.finish()
    og_in.arrive()

    result_out = Outbound(p, links, g.result_low, g.result_home)

    def hidden_stage(inner_ref, hidden_ref, low_ref, total_ref):
        second = g.n2[...] * g.cross_gain[...] + g.cross_shift[...]
        low_ref[...] = second.astype(BF16)
        total_ref[...] = second + g.contract_bias[...]

        def forward(z, carry):
            bias = g.expand_bias[:, pl.ds(pl.multiple_of(z * hid, PAIR), hid)]
            inner = dot_nn(low_ref[...], flat_rows(g.w_hidden[z, :, :, :hid])) + bias
            inner_ref[z] = inner
            hidden = (inner * jax.nn.sigmoid(inner)).astype(BF16)
            hidden_ref[z] = hidden
            total_ref[...] += dot_nt(hidden, flat_rows(g.w_hidden[z, :, :, hid:]))
            return carry

        lax.fori_loop(0, cols, forward, 0)
        normed, inverse = norm_forward(total_ref[...])
        g.result_low[...] = (normed * g.final_gain[...] + g.final_shift[...]).astype(BF16)
        result_out.start()
        gradient = g.og[...].astype(F32)
        g.small[0, 0:1, :] = column_sum(gradient * normed)
        g.small[0, 1:2, :] = column_sum(gradient)
        third = norm_backward(gradient, normed, inverse, g.final_gain[...])
        g.small[0, 2:3, :] = column_sum(third)
        third_low = third.astype(BF16)
        total_ref[...] = third

        def backward(z, carry):
            inner = inner_ref[z]
            hidden_back = dot_nn(third_low, flat_rows(g.w_hidden[z, :, :, hid:]))
            g.g_hidden[z, :, :, hid:] = row_blocks(dot_tn(third_low, hidden_ref[z]), row_count)
            logistic = jax.nn.sigmoid(inner)
            inner_back = (hidden_back * logistic * (1.0 + inner * (1.0 - logistic))).astype(BF16)
            g.small[0, pl.ds(13 + z, 1), :] = column_sum(inner_back.astype(F32))
            g.g_hidden[z, :, :, :hid] = row_blocks(dot_tn(low_ref[...], inner_back), row_count)
            total_ref[...] += dot_nt(inner_back, flat_rows(g.w_hidden[z, :, :, :hid]))
            return carry

        lax.fori_loop(0, cols, backward, 0)
        gradient = total_ref[...]
        normed = g.n2[...]
        g.small[0, 3:4, :] = column_sum(gradient * normed)
        g.small[0, 4:5, :] = column_sum(gradient)
        second_grad = norm_backward(gradient, normed, g.i2[:, 0:1], g.cross_gain[...])
        g.small[0, 5:6, :] = column_sum(second_grad)
        g.grad[...] = second_grad

    pl.run_scoped(
        hidden_stage,
        pltpu.VMEM((cols, own, hid), F32),
        pltpu.VMEM((cols, own, hid), BF16),
        pltpu.VMEM((own, width), BF16),
        pltpu.VMEM((own, width), F32),
    )
    put_hidden = Reduce(p, links, g.g_hidden, g.p_hidden, g.q_hidden, g.c_hidden, g.r_hidden)
    put_hidden.start()
    put_back = Reduce(p, links, g.g_back, g.p_back, g.q_back, g.c_back, g.r_back)
    put_enc = Reduce(p, links, g.g_enc, g.p_enc, g.q_enc, g.c_enc, g.r_enc)
    put_self = Reduce(p, links, g.g_self, g.p_self, g.q_self, g.c_self, g.r_self)
    enc_out = Outbound(p, links, g.enc_low, g.enc_home)
    tok_out = Outbound(p, links, g.tok_low, g.tok_home)

    def trade(acc_ref, stage_ref, arrive_ref):
        for i in range(2):
            stage_ref[i, :, 0:part, :] = acc_ref[i, :, pl.ds(other_low, part), :].astype(BF16)
            stage_ref[i, :, part:own, :] = acc_ref[i, :, pl.ds(other_high, part), :].astype(BF16)
        return links.start(stage_ref, arrive_ref, p.partner)

    def joined(acc_ref, arrive_ref, i, z):
        mine_rows = jnp.concatenate(
            [acc_ref[i, z, pl.ds(low_at, part), :], acc_ref[i, z, pl.ds(high_at, part), :]],
            axis=0,
        )
        return (mine_rows + arrive_ref[i, z].astype(F32)).astype(BF16)

    def back_stage(cross_acc, self_acc):
        grad_low = g.grad[...].astype(BF16)
        for z in range(cols):
            g.g_back[z, :, :, 2 * PAIR :] = row_blocks(dot_tn(grad_low, g.cmixed[z]), row_count)
            g.mixed_back[z] = dot_nn(grad_low, attn_w(z, 4)).astype(BF16)
        cross_acc[...] = jnp.zeros_like(cross_acc)
        for block in range(2):
            attend_block_back(
                g.cq,
                g.ckv,
                g.cmixed,
                g.clse,
                g.mixed_back,
                g.dq,
                cross_acc,
                block * part,
                part,
                span,
                own,
                source_mask_back,
            )
            if block == 0:
                put_hidden.after_pair()
        ckv_trade = trade(cross_acc, g.stage_cross, g.arrive_cross)
        put_hidden.after_plane(0)
        normed = g.n1[...]
        first_low = (normed * g.attn_gain[...] + g.attn_shift[...]).astype(BF16)
        gradient = g.grad[...]
        for z in range(cols):
            dq = g.dq[z]
            g.g_back[z, :, :, PAIR : 2 * PAIR] = row_blocks(dot_tn(first_low, dq), row_count)
            g.small[0, 11:12, z * PAIR : (z + 1) * PAIR] = column_sum(dq.astype(F32))
            gradient = gradient + dot_nt(dq, attn_w(z, 1))
        g.small[0, 6:7, :] = column_sum(gradient * normed)
        g.small[0, 7:8, :] = column_sum(gradient)
        first_grad = norm_backward(gradient, normed, g.i1[:, 0:1], g.attn_gain[...])
        g.small[0, 8:9, :] = column_sum(first_grad)
        g.grad[...] = first_grad
        grad_low = first_grad.astype(BF16)
        for z in range(cols):
            g.g_back[z, :, :, 0:PAIR] = row_blocks(dot_tn(grad_low, g.mixed[z]), row_count)
            g.mixed_back[z] = dot_nn(grad_low, attn_w(z, 0)).astype(BF16)
        put_back.start()

        ckv_trade.wait_recv()
        e = g.e[...]
        for z in range(cols):
            dk = joined(cross_acc, g.arrive_cross, 0, z)
            dv = joined(cross_acc, g.arrive_cross, 1, z)
            g.small[0, 12:13, z * PAIR : (z + 1) * PAIR] = column_sum(dv.astype(F32))
            both = jnp.concatenate([dk, dv], axis=1)
            g.g_enc[z] = row_blocks(dot_tn(e, both), row_count)
            term = dot_nt(both, attn_w(z, 2, 2))
            total = term if z == 0 else total + term
        g.enc_low[...] = total.astype(BF16)
        enc_out.start()
        put_enc.start()
        for level in range(1, len(p.plane_bits)):
            put_hidden.after_plane(level)

        self_acc[...] = jnp.zeros_like(self_acc)
        for block in range(2):
            for parity in range(2):

                @pl.when(p.core == parity)
                def _():
                    keys = (4 - parity if block else parity + 1) * part
                    attend_block_back(
                        g.q,
                        g.kv,
                        g.mixed,
                        g.lse,
                        g.mixed_back,
                        g.dq,
                        self_acc,
                        block * part,
                        part,
                        keys,
                        part,
                        causal_last_back(part, keys),
                    )

            if block == 0:
                put_back.after_pair()
                put_enc.after_pair()
        kv_trade = trade(self_acc, g.stage_self, g.arrive_self)
        for level in range(len(p.plane_bits)):
            put_back.after_plane(level)
            put_enc.after_plane(level)
        kv_trade.wait_recv()
        x = g.x[...]
        total = g.grad[...]
        for z in range(cols):
            dq = g.dq[z]
            dk = joined(self_acc, g.arrive_self, 0, z)
            dv = joined(self_acc, g.arrive_self, 1, z)
            g.small[0, 9:10, z * PAIR : (z + 1) * PAIR] = column_sum(dq.astype(F32))
            g.small[0, 10:11, z * PAIR : (z + 1) * PAIR] = column_sum(dv.astype(F32))
            both = jnp.concatenate([dq, dk, dv], axis=1)
            g.g_self[z] = row_blocks(dot_tn(x, both), row_count)
            total = total + dot_nt(both, self_w(z))
        g.tok_low[...] = total.astype(BF16)

        tok_out.start()
        put_self.start()
        total = Total(p, links, g.small, g.small_arrived)
        total.start()
        put_hidden.finish()
        put_back.finish()
        put_enc.finish()
        put_self.after_pair()
        total.step()
        for level in range(len(p.plane_bits)):
            put_self.after_plane(level)
            total.step()
        g.r_small[...] = total.finish()
        put_self.finish()
        for moved in (result_out, enc_out, tok_out):
            moved.arrive()
            moved.drain()
        for moved in (x_in, e_in, og_in):
            moved.drain()
        links.drain()

    count = g.small.shape[1]
    g.small[0, 13 + cols : count, :] = jnp.zeros((count - 13 - cols, width), F32)
    pl.run_scoped(
        back_stage,
        pltpu.VMEM((2, cols, span, PAIR), F32),
        pltpu.VMEM((2, cols, span, PAIR), F32),
    )


def finish_kernel(width, names, out_names, *refs):
    g = named(names, refs[: len(names)])
    homes, o = refs[len(names) : len(names) + 3], named(out_names, refs[len(names) + 3 :])
    for home, source in zip(homes, (g.result_home, g.tok_home, g.enc_home)):
        home[...] = source[...].astype(F32)
    hid = o.expand.shape[1]

    def block(ref, at):
        return ref[:, at * PAIR : (at + 1) * PAIR]

    o.self_query[...] = block(g.r_self, 0)
    o.self_key[...] = block(g.r_self, 1)
    o.self_value[...] = block(g.r_self, 2)
    o.self_output[...] = jnp.transpose(block(g.r_back, 0))
    o.cross_query[...] = block(g.r_back, 1)
    o.cross_output[...] = jnp.transpose(block(g.r_back, 2))
    o.cross_key[...] = block(g.r_enc, 0)
    o.cross_value[...] = block(g.r_enc, 1)
    o.expand[...] = g.r_hidden[:, :hid]
    o.contract[...] = jnp.transpose(g.r_hidden[:, hid:])
    vectors = (
        o.final_gain,
        o.final_shift,
        o.contract_bias,
        o.cross_gain,
        o.cross_shift,
        o.cross_output_bias,
        o.attn_gain,
        o.attn_shift,
        o.self_output_bias,
        o.self_query_bias,
        o.self_value_bias,
        o.cross_query_bias,
        o.cross_value_bias,
    )
    for i, vector in enumerate(vectors):
        vector[...] = g.r_small[i : i + 1, :]
    at = len(vectors)
    for z in range(o.expand_bias.shape[1] // width):
        o.expand_bias[:, z * width : (z + 1) * width] = g.r_small[at + z : at + z + 1, :]


def per_device(
    tokens,
    encoded,
    source_len,
    out_grad,
    self_query,
    self_key,
    self_value,
    self_output,
    self_query_bias,
    self_value_bias,
    self_output_bias,
    cross_query,
    cross_key,
    cross_value,
    cross_output,
    cross_query_bias,
    cross_value_bias,
    cross_output_bias,
    expand,
    expand_bias,
    contract,
    contract_bias,
    attn_gain,
    attn_shift,
    cross_gain,
    cross_shift,
    final_gain,
    final_shift,
):
    inputs = dict(locals())
    row_count = lax.axis_size(ROW)
    cols = lax.axis_size(COL)
    micro_count, part, width = tokens.shape
    depth, head_width = self_query.shape
    hid = expand.shape[1]
    assert micro_count == 2 and cols == 4 and source_len.shape[1] == 1
    assert head_width == PAIR and row_count % 4 == 0 and hid == width
    own = 2 * part
    plane = row_count // 2
    small_rows = -(-(13 + cols) // 8) * 8
    small_steps = len(bits_of(row_count - 1)) + len(bits_of(cols - 1))
    links = 3 * (cols - 1 + 2 * (plane - 1) + 2 * plane)
    links += 4 * (plane + 2 * (plane - 1) + cols - 1) + small_steps
    links += 6 * 2 + 1 + 4 + 2

    def whole(columns):
        return pltpu.VMEM((cols, row_count, depth, columns), BF16)

    def from_pair(columns):
        return pltpu.VMEM((plane, cols, depth, columns), BF16)

    def from_plane(columns):
        return pltpu.VMEM((2 * (plane - 1), cols // 2, depth, columns), BF16)

    def from_col(columns):
        return pltpu.VMEM((cols - 1, depth, columns), BF16)

    rows_low = pltpu.VMEM((own, width), BF16)
    rows_f32 = pltpu.VMEM((own, width), F32)
    stat_f32 = pltpu.VMEM((own, PAIR), F32)
    heads_low = pltpu.VMEM((cols, own, PAIR), BF16)
    heads_f32 = pltpu.VMEM((cols, own, PAIR), F32)
    keys_low = pltpu.VMEM((2, cols, 2 * own, PAIR), BF16)
    half_keys = pltpu.VMEM((2, cols, own, PAIR), BF16)
    lengths = pltpu.VMEM((2, 8, PAIR), jnp.int32)
    scratch = dict(
        x=rows_low,
        e=rows_low,
        og=rows_low,
        og_low=pltpu.VMEM((2, part, width), BF16),
        pack_self=pltpu.VMEM((depth, 3 * PAIR), BF16),
        pack_attn=pltpu.VMEM((depth, 5 * PAIR), BF16),
        pack_hidden=pltpu.VMEM((depth, 2 * hid), BF16),
        w_self=whole(3 * PAIR),
        w_attn=whole(5 * PAIR),
        w_hidden=whole(2 * hid),
        len_own=lengths,
        len_other=lengths,
        q=heads_low,
        kv=keys_low,
        ckv=keys_low,
        mixed=heads_low,
        lse=heads_f32,
        n1=rows_f32,
        i1=stat_f32,
        cq=heads_low,
        cmixed=heads_low,
        clse=heads_f32,
        n2=rows_f32,
        i2=stat_f32,
        grad=rows_f32,
        mixed_back=heads_low,
        dq=heads_low,
        result_low=rows_low,
        enc_low=rows_low,
        tok_low=rows_low,
        stage_cross=half_keys,
        arrive_cross=half_keys,
        stage_self=half_keys,
        arrive_self=half_keys,
        small=pltpu.VMEM((2, small_rows, width), F32),
        small_arrived=pltpu.VMEM((small_steps, small_rows, width), F32),
        g_hidden=whole(2 * hid),
        p_hidden=from_pair(2 * hid),
        q_hidden=from_plane(2 * hid),
        c_hidden=from_col(2 * hid),
        g_back=whole(3 * PAIR),
        p_back=from_pair(3 * PAIR),
        q_back=from_plane(3 * PAIR),
        c_back=from_col(3 * PAIR),
        g_enc=whole(2 * PAIR),
        p_enc=from_pair(2 * PAIR),
        q_enc=from_plane(2 * PAIR),
        c_enc=from_col(2 * PAIR),
        g_self=whole(3 * PAIR),
        p_self=from_pair(3 * PAIR),
        q_self=from_plane(3 * PAIR),
        c_self=from_col(3 * PAIR),
        send=pltpu.SemaphoreType.DMA((links,)),
        recv=pltpu.SemaphoreType.DMA((links,)),
    )
    home = jax.ShapeDtypeStruct((2, part, width), BF16)
    outs = dict(
        result_home=(home, ANY_SPEC),
        tok_home=(home, ANY_SPEC),
        enc_home=(home, ANY_SPEC),
        r_self=(jax.ShapeDtypeStruct((depth, 3 * PAIR), F32), VMEM_SPEC),
        r_back=(jax.ShapeDtypeStruct((depth, 3 * PAIR), F32), VMEM_SPEC),
        r_enc=(jax.ShapeDtypeStruct((depth, 2 * PAIR), F32), VMEM_SPEC),
        r_hidden=(jax.ShapeDtypeStruct((depth, 2 * hid), F32), VMEM_SPEC),
        r_small=(jax.ShapeDtypeStruct((small_rows, width), F32), VMEM_SPEC),
    )
    names = tuple(inputs)
    specs = [ANY_SPEC, ANY_SPEC, SMEM_SPEC] + [VMEM_SPEC] * (len(names) - 3)
    moved = pl.pallas_call(
        functools.partial(layer_kernel, row_count, cols, names + tuple(outs) + tuple(scratch)),
        out_shape=[shape for shape, _ in outs.values()],
        in_specs=specs,
        out_specs=[spec for _, spec in outs.values()],
        scratch_shapes=list(scratch.values()),
        compiler_params=pltpu.CompilerParams(
            collective_id=0, has_side_effects=True, vmem_limit_bytes=VMEM_LIMIT
        ),
        name="layer",
    )(*(v.reshape(1, -1) if v.ndim == 1 else v for v in inputs.values()))
    shapes = [(2, part, width)] * 3 + [inputs[n].shape for n in names[4:]]
    final = pl.pallas_call(
        functools.partial(finish_kernel, width, tuple(outs), names[4:]),
        out_shape=[
            jax.ShapeDtypeStruct((1,) + shape if len(shape) == 1 else shape, F32)
            for shape in shapes
        ],
        in_specs=[VMEM_SPEC] * len(outs),
        out_specs=[VMEM_SPEC] * len(shapes),
        compiler_params=pltpu.CompilerParams(vmem_limit_bytes=VMEM_LIMIT),
        name="finish",
    )(*moved)
    return tuple(v.reshape(-1) if v.shape[0] == 1 else v for v in final)


def solution(mesh):
    tokens, down, across, same = P(None, AXES, None), P(ROW, COL), P(COL, ROW), P()
    attention = (down, down, down, across, same, same, same)
    weights = attention * 2 + (down, same, across) + (same,) * 7
    return jax.shard_map(
        per_device,
        mesh=mesh,
        in_specs=(tokens, tokens, P(None, ROW), tokens) + weights,
        out_specs=(tokens, tokens, tokens) + weights,
        check_vma=False,
    )
```

time: 1060 us -> 186 us (0.18)
  waiting for transfers between devices: 501 us -> 0 us
  matrix products: 199 us -> 0 us
  Pallas kernels: 0 us -> 176 us
  blocking collectives: 133 us -> 0 us
  other arithmetic: 97.6 us -> 0 us
  local copies, waits for them, and re-layouts: 47.8 us -> 8.85 us
  loops' own time: 29.1 us -> 0 us
  starting transfers between devices: 25.5 us -> 0 us
  between operations: 17 us -> 0.71 us
    reduce_scatter x14 -> x0, waiting for transfers between devices: 333 us -> none  [the longest x6 227 us: spread(): lax.psum_scatter(partial_term(jnp.int32(0), left_side.shape[0] // lax.axi...]
    dot_general x116 -> x0, matrix products: 199 us -> none  [the longest x20 36.3 us: product(): return jnp.dot(left_side, right_side, preferred_element_type=jnp.float32)]
    pallas_call x0 -> x2, Pallas kernels: none -> 176 us  [the longest x1 172 us: per_device(): pl.pallas_call(functools.partial(layer_kernel, row_count, cols, names + t...]
    all_gather x14 -> x0, waiting for transfers between devices: 156 us -> none  [the longest x6 72 us: collect_grads(): return lax.all_gather(values, 'col', axis=0, tiled=True)]
    all_gather x10 -> x0, blocking collectives: 92.6 us -> none  [the longest x1 10.9 us: fetch_blocks(): lax.all_gather(self_query, 'row', axis=0, tiled=True)]
    reduce_sum x37 -> x0, other arithmetic: 46.2 us -> none  [the longest x8 7.95 us: one_block(): summed = jnp.sum(raised, axis=-1, keepdims=True)]
    psum x1 -> x0, blocking collectives: 40.7 us -> none  [per_device(): lax.psum((place(small[0], model_width), place(small[1], model_width), sma...]
    another operation x8 -> x0, loops' own time: 29.1 us -> none  [the longest x4 21 us: attend_back(): lax.scan(one_block, (empty, empty), (query_blocks, grad_blocks, log_total...]
  transfers between devices with their start and end apart: 34 -> 0, of which waited for: 22 -> 0; matrix products, arithmetic and copies ran while one was open for 29% -> 0% of each run, Pallas kernels for 0% -> 0%
where the time goes in v1:
time: 186 us
  Pallas kernels  176 us (95%)
  local copies, waits for them, and re-layouts  8.85 us (5%)
    pallas_call x1, Pallas kernels, per_device(): pl.pallas_call(functools.partial(layer_kernel, row_count, cols, names + t...  172 us
    unnamed x11, local copies, waits for them, and re-layouts  8.85 us

profile of v1, /device:TPU:0, one launch (start us, length us, event | category | flops | bytes accessed | tf_op | source)
XLA Modules:
  0.0 185.5 jit_solution(12631401068778092928)
XLA Ops:
  0.7 0.0 copy-start.1
  0.7 1.3 copy.55.refs_2_
  2.0 1.4 copy.56.refs_7_
  3.4 1.4 copy.57.refs_14_
  4.9 0.0 copy-done.1
  4.9 0.8 copy.58.refs_20_
  5.6 172.3 %layer.1 = (bf16[2,256,512]{2,1,0:T(8,128)(2,1)}, bf16[2,256,512]{2,1,0:T(8,128)(2,1)}, bf16[2,256,512]{2,1,0:T(8,128)(2,1)}, f32[64,384]{1,0:T(8,128)}, f32[64,...) custom-call(bf16[2,256,512]{2,1,0:T(8,128)(2,1)} %refs_0_.1, ...), custom_call_target="tpu_custom_call" | custom-call | tf_op jit(solution)/shard_map/layer/pallas_call | solution.py:1108
  178.0 3.7 %finish.1 = (f32[2,256,512]{2,1,0:T(8,128)}, f32[2,256,512]{2,1,0:T(8,128)}, f32[2,256,512]{2,1,0:T(8,128)}, f32[64,128]{1,0:T(8,128)}, f32[64,128]{1,0:T(8,128)...) custom-call(bf16[2,256,512]{2,1,0:T(8,128)(2,1)} %get-tuple-element., ...), custom_call_target="tpu_custom_call" | custom-call | tf_op jit(solution)/shard_map/finish/pallas_call | solution.py:1120
  181.6 0.0 copy-start
  181.6 1.6 copy.59
  183.2 1.5 copy.60
  184.8 0.0 copy-done
  184.8 0.8 copy.61
Async XLA Ops:
  0.7 4.2 %copy-start.1 = (bf16[512,64]{0,1:T(8,128)(2,1)S(1)}, bf16[512,64]{0,1:T(8,128)(2,1)}, u32[]{:S(2)}) copy-start(bf16[512,64]{0,1:T(8,128)(2,1)} %param.48) | copy-start | bytes 196612
  181.6 3.1 %copy-start = (f32[512,64]{1,0:T(8,128)S(1)}, f32[512,64]{1,0:T(8,128)}, u32[]{:S(2)}) copy-start(f32[512,64]{1,0:T(8,128)} %get-tuple-element.116) | copy-start | bytes 393220

commit v2 on v1

--- a/solution.py
+++ b/solution.py
@@ -62,7 +62,7 @@
     return first, (1.0 - first)
 
 
-def attend_block(q_ref, kv_ref, out_ref, lse_ref, row0, rows, span, mask):
+def attend_block(q_ref, kv_ref, out_ref, lse_ref, row0, rows, span, mask, pairs):
     first, second = lane_masks()
     halves = (first.astype(BF16), second.astype(BF16))
 
@@ -85,11 +85,23 @@
         )
         return carry
 
-    lax.fori_loop(0, q_ref.shape[0], one_pair, 0)
+    lax.fori_loop(pairs[0], pairs[1], one_pair, 0)
 
 
 def attend_block_back(
-    q_ref, kv_ref, mixed_ref, lse_ref, grad_ref, dq_ref, dkv_ref, row0, rows, span, chunk, mask
+    q_ref,
+    kv_ref,
+    mixed_ref,
+    lse_ref,
+    grad_ref,
+    dq_ref,
+    dkv_ref,
+    row0,
+    rows,
+    span,
+    chunk,
+    mask,
+    pairs,
 ):
     first, second = lane_masks()
     halves = (first.astype(BF16), second.astype(BF16))
@@ -126,7 +138,7 @@
         ) * jnp.asarray(HEAD_DIM**-0.5, BF16)
         return carry
 
-    lax.fori_loop(0, q_ref.shape[0], one_pair, 0)
+    lax.fori_loop(pairs[0], pairs[1], one_pair, 0)
 
 
 def causal_last(rows, span):
@@ -178,7 +190,7 @@
 
 class Links:
     def __init__(self, send, recv):
-        self.send, self.recv, self.count, self.open = send, recv, 0, []
+        self.send, self.recv, self.count = send, recv, 0
 
     def take(self, amount=1):
         at = self.count
@@ -194,18 +206,6 @@
             device_id=device,
             device_id_type=MESH,
         )
-
-    def start(self, src, dst, device):
-        at = self.take()
-        copy = self.copy(src, dst, device, at, at)
-        copy.start()
-        self.open.append(copy)
-        return copy
-
-    def drain(self):
-        for copy in self.open:
-            copy.wait_send()
-        self.open = []
 
 
 class Place:
@@ -386,82 +386,199 @@
 
 
 class Gather:
-    def __init__(self, place, links, shard, whole):
+    def __init__(self, place, links, shard, whole, relayed):
         self.place, self.links, self.shard, self.whole = place, links, shard, whole
-        self.plane, self.pair = {}, []
+        self.relayed = relayed
+        self.along_at = links.take(2 * (place.cols - 1))
+        self.base = {}
+        for m in place.members:
+            if m:
+                self.base[(False, m)] = links.take(place.cols)
+            self.base[(True, m)] = links.take()
+        self.orders = (place.plane_bits, place.plane_bits[::-1])
+        whole[place.col, place.row] = shard[...]
+
+    def sources(self, step):
+        p = self.place
+        if step == 0:
+            return [(p.col, None, 0)]
+        if not self.relayed:
+            return [(flipped(p.col, bits_of(step)), None, 0)]
+        return [
+            (p.col - step, p.col >= step, 1),
+            (p.col + step, p.col + step < p.cols, -1),
+        ]
+
+    def guarded(self, valid, action):
+        if valid is None:
+            action()
+        else:
+            pl.when(valid)(action)
+
+    def hop(self, step, column, direction):
+        p = self.place
+        block = self.whole.at[column, p.row]
+        if not self.relayed:
+            at = self.along_at + step - 1
+            return self.links.copy(block, block, (p.row, flipped(p.col, bits_of(step))), at, at)
+        at = self.along_at + 2 * (step - 1) + (0 if direction > 0 else 1)
+        return self.links.copy(block, block, (p.row, p.col + direction), at, at)
+
+    def forward(self, step, column, direction, act):
+        p = self.place
+        if not self.relayed:
+            for far in range(1, p.cols if step == 0 else 0):
+                act(self.hop(far, column, 0))
+            return
+        if step + 1 >= p.cols:
+            return
+        for way in (1, -1) if step == 0 else (direction,):
+            room = p.col + 1 < p.cols if way > 0 else p.col > 0
+
+            @pl.when(room)
+            def _(way=way):
+                act(self.hop(step + 1, column, way))
+
+    def plane_copy(self, column, m, bit):
+        p = self.place
+        block = self.whole.at[column, flipped(p.row, bits_of(m))]
+        at = self.base[(False, m + bit)] + column
+        return self.links.copy(block, block, (flipped(p.row, [bit]), p.col), at, at)
+
+    def pair_copy(self, m):
+        p = self.place
+        block = self.whole.at[:, flipped(p.row, bits_of(m))]
+        at = self.base[(True, m)]
+        return self.links.copy(block, block, p.partner, at, at)
+
+    def to_pair(self, level):
+        for m in self.place.members:
+            if len(bits_of(m)) == level:
+                self.pair_copy(m).start()
+
+    def outgoing(self, step, column, m):
+        order = self.orders[step % 2]
+        reached = max([order.index(b) for b in bits_of(m)], default=-1)
+        return [self.plane_copy(column, m, bit) for bit in order[reached + 1 :]]
 
     def start(self):
         p = self.place
-        self.along = [
-            self.links.start(
-                self.shard, self.whole.at[p.col, p.row], (p.row, flipped(p.col, bits_of(k)))
+        self.forward(0, p.col, 0, lambda c: c.start())
+
+    def start_plane(self):
+        for copy in self.outgoing(0, self.place.col, 0):
+            copy.start()
+
+    def step(self, step):
+        for column, valid, direction in self.sources(step):
+
+            def action(column=column, direction=direction):
+                self.hop(step, column, direction).wait_recv()
+                self.forward(step, column, direction, lambda c: c.start())
+                for copy in self.outgoing(step, column, 0):
+                    copy.start()
+
+            self.guarded(valid, action)
+
+    def arrived(self, column, m, order):
+        bit = max(bits_of(m), key=order.index)
+        return self.plane_copy(column, m - bit, bit)
+
+    def plane(self, step, level):
+        order = self.orders[step % 2]
+        for column, valid, _ in self.sources(step):
+
+            def action(column=column):
+                for m in self.place.members:
+                    if len(bits_of(m)) == level:
+                        self.arrived(column, m, order).wait_recv()
+                        for copy in self.outgoing(step, column, m):
+                            copy.start()
+
+            self.guarded(valid, action)
+
+    def planes_from(self, step, first):
+        for level in range(first, len(self.place.plane_bits) + 1):
+            self.plane(step, level)
+
+    def each(self, visit):
+        p = self.place
+        for step in range(p.cols):
+            for column, valid, direction in self.sources(step):
+                self.guarded(
+                    valid, functools.partial(visit, step=step, column=column, direction=direction)
+                )
+
+    def finish(self):
+        for m in self.place.members:
+            self.pair_copy(m).wait_recv()
+
+    def drain(self):
+        for m in self.place.members:
+            self.pair_copy(m).wait_send()
+
+        def visit(step, column, direction):
+            self.forward(step, column, direction, lambda c: c.wait_send())
+            for m in self.place.members:
+                for copy in self.outgoing(step, column, m):
+                    copy.wait_send()
+
+        self.each(visit)
+
+
+class Reduce:
+    def __init__(self, place, links, grads, from_pair, from_plane, from_col, total, out, relayed):
+        self.place, self.links, self.grads = place, links, grads
+        self.relayed = relayed
+        self.sums, self.from_plane, self.from_col = from_pair, from_plane, from_col
+        self.total, self.out = total, out
+        self.moves = []
+        for side_at, (_, order) in enumerate(place.sides):
+            for level in range(len(order)):
+                for m in subsets(order[level + 1 :]):
+                    self.moves.append((side_at, level, m))
+        self.pair_at = links.take(len(place.members) * (place.cols if relayed else 1))
+        self.plane_at = links.take(len(self.moves))
+        self.along_at = links.take(2 * (place.cols - 1))
+        self.out_at = links.take()
+
+    def pair_copy(self, at, m, column=None):
+        p = self.place
+        if column is not None:
+            sem = self.pair_at + at * p.cols + column
+            return self.links.copy(
+                self.grads.at[column, flipped(p.row, [1] + bits_of(m))],
+                self.sums.at[at, column],
+                p.partner,
+                sem,
+                sem,
             )
-            for k in range(1, p.cols)
-        ]
-        self.whole[p.col, p.row] = self.shard[...]
-
-    def block(self, side, m):
-        p = self.place
-        return self.whole.at[pl.ds(side, p.half), flipped(p.row, bits_of(m))]
-
-    def send_out(self, side, order, m):
-        p = self.place
-        reached = max([order.index(b) for b in bits_of(m)], default=-1)
-        here = self.block(side, m)
-        for bit in order[reached + 1 :]:
-            self.plane[(side, m + bit)] = self.links.start(
-                here, here, (flipped(p.row, [bit]), p.col)
-            )
-        self.pair.append(self.links.start(here, here, p.partner))
-
-    def after_col(self):
-        for copy in self.along:
-            copy.wait_recv()
-        for side, order in self.place.sides:
-            self.send_out(side, order, 0)
-
-    def after_plane(self, level):
-        for side, order in self.place.sides:
-            for m in self.place.members:
-                if len(bits_of(m)) == level:
-                    self.plane[(side, m)].wait_recv()
-                    self.send_out(side, order, m)
-
-    def after_planes(self):
-        for level in range(1, len(self.place.plane_bits) + 1):
-            self.after_plane(level)
-
-    def finish(self):
-        for copy in self.pair:
-            copy.wait_recv()
-
-
-class Reduce:
-    def __init__(self, place, links, grads, from_pair, from_plane, from_col, out):
-        self.place, self.links, self.grads = place, links, grads
-        self.sums, self.from_plane, self.from_col, self.out = from_pair, from_plane, from_col, out
-        at = 0
-        self.bases = []
-        for _, order in place.sides:
-            bases = []
-            for level in range(len(order)):
-                bases.append(at)
-                at += len(subsets(order[level + 1 :]))
-            self.bases.append(bases)
+        return self.links.copy(
+            self.grads.at[:, flipped(p.row, [1] + bits_of(m))],
+            self.sums.at[at],
+            p.partner,
+            self.pair_at + at,
+            self.pair_at + at,
+        )
+
+    def pair_copies(self, at, m):
+        if self.relayed:
+            return [self.pair_copy(at, m, column) for column in range(self.place.cols)]
+        return [self.pair_copy(at, m)]
 
     def start(self):
-        p = self.place
-        self.pair = [
-            self.links.start(
-                self.grads.at[:, flipped(p.row, [1] + bits_of(m))], self.sums.at[at], p.partner
-            )
-            for at, m in enumerate(p.members)
-        ]
+        for at, m in enumerate(self.place.members):
+            self.pair_copy(at, m).start()
+
+    def start_column(self, column):
+        for at, m in enumerate(self.place.members):
+            self.pair_copy(at, m, column).start()
 
     def after_pair(self):
         p = self.place
         for at, m in enumerate(p.members):
-            self.pair[at].wait_recv()
+            for copy in self.pair_copies(at, m):
+                copy.wait_recv()
             own_row = flipped(p.row, bits_of(m))
 
             def body(i, carry, at=at, own_row=own_row):
@@ -471,88 +588,202 @@
                 return carry
 
             lax.fori_loop(0, p.cols, body, 0)
-        self.moving = [self.send(side, 0) for side in range(2)]
-
-    def send(self, side_at, level):
-        p = self.place
+        self.send(0)
+
+    def plane_copy(self, at):
+        p = self.place
+        side_at, level, m = self.moves[at]
         side, order = p.sides[side_at]
         bit = order[level]
-        batch = []
-        for slot, m in enumerate(subsets(order[level + 1 :])):
-            at = self.bases[side_at][level] + slot
-            copy = self.links.start(
-                self.sums.at[p.members.index(m + bit), pl.ds(side, p.half)],
-                self.from_plane.at[at],
-                (flipped(p.row, [bit]), p.col),
+        return self.links.copy(
+            self.sums.at[p.members.index(m + bit), pl.ds(side, p.half)],
+            self.from_plane.at[at],
+            (flipped(p.row, [bit]), p.col),
+            self.plane_at + at,
+            self.plane_at + at,
+        )
+
+    def at_level(self, level):
+        return [at for at, move in enumerate(self.moves) if move[1] == level]
+
+    def send(self, level):
+        for at in self.at_level(level):
+            self.plane_copy(at).start()
+
+    def after_plane(self, level):
+        p = self.place
+        for at in self.at_level(level):
+            side_at, _, m = self.moves[at]
+            self.plane_copy(at).wait_recv()
+            into, side = p.members.index(m), p.sides[side_at][0]
+
+            def body(i, carry, into=into, at=at, side=side):
+                self.sums[into, side + i] = (
+                    self.sums[into, side + i].astype(F32) + self.from_plane[at, i].astype(F32)
+                ).astype(BF16)
+                return carry
+
+            lax.fori_loop(0, p.half, body, 0)
+        if level + 1 < len(p.plane_bits):
+            self.send(level + 1)
+        else:
+            for step in range(1, 2 if self.relayed else p.cols):
+                self.hops(step, lambda c: c.start())
+
+    def hop(self, step, way, column):
+        p = self.place
+        if not self.relayed:
+            at = self.along_at + step - 1
+            return self.links.copy(
+                self.sums.at[0, column], self.from_col.at[step - 1], (p.row, column), at, at
             )
-            batch.append((m, at, copy))
-        return batch
-
-    def after_plane(self, level):
-        p = self.place
-        last = level + 1 == len(p.plane_bits)
-        for side_at in range(2):
-            side = p.sides[side_at][0]
-            for m, at, copy in self.moving[side_at]:
-                copy.wait_recv()
-                into = p.members.index(m)
-
-                def body(i, carry, into=into, at=at, side=side):
-                    self.sums[into, side + i] = (
-                        self.sums[into, side + i].astype(F32)
-                        + self.from_plane[at, i].astype(F32)
-                    ).astype(BF16)
-                    return carry
-
-                lax.fori_loop(0, p.half, body, 0)
-            if not last:
-                self.moving[side_at] = self.send(side_at, level + 1)
-        if last:
-            self.along = []
+        slot = 2 * (step - 1) + (0 if way > 0 else 1)
+        at = self.along_at + slot
+        return self.links.copy(
+            self.sums.at[0, column], self.from_col.at[slot], (p.row, p.col + way), at, at
+        )
+
+    def hops(self, step, act):
+        p = self.place
+        if not self.relayed:
+            act(self.hop(step, 0, flipped(p.col, bits_of(step))))
+            return
+        for way in (1, -1):
+            here = p.col if way > 0 else p.cols - 1 - p.col
+            column = p.cols + p.col - step if way > 0 else p.col - p.cols + step
+            inner = p.col + 1 < p.cols if way > 0 else p.col > 0
+
+            @pl.when(jnp.logical_and(here < step, inner))
+            def _(way=way, column=column, step=step):
+                act(self.hop(step, way, column))
+
+    def step(self, step):
+        p = self.place
+        for way in (1, -1):
+            here = p.col if way > 0 else p.cols - 1 - p.col
+            column = p.cols + p.col - 1 - step if way > 0 else p.col - p.cols + 1 + step
+            slot = 2 * (step - 1) + (0 if way > 0 else 1)
+
+            @pl.when(jnp.logical_and(here >= 1, here <= step))
+            def _(way=way, column=column, slot=slot):
+                self.hop(step, way, column).wait_recv()
+                self.sums[0, column] = (
+                    self.sums[0, column].astype(F32) + self.from_col[slot].astype(F32)
+                ).astype(BF16)
+
+        if step + 1 < p.cols:
+            self.hops(step + 1, lambda c: c.start())
+
+    def out_copy(self):
+        return pltpu.make_async_copy(self.total, self.out, self.links.recv.at[self.out_at])
+
+    def finish(self, done=0):
+        p = self.place
+        last = p.cols - 1
+        if not self.relayed:
+            total = self.sums[0, p.col].astype(F32)
+            for step in range(1, p.cols):
+                self.hop(step, 0, flipped(p.col, bits_of(step))).wait_recv()
+                total = total + self.from_col[step - 1].astype(F32)
+            self.total[...] = total
+        else:
+            for step in range(done + 1, last):
+                self.step(step)
+            self.total[...] = self.sums[0, p.col].astype(F32)
+            for way in (1, -1):
+                here = p.col if way > 0 else p.cols - 1 - p.col
+                slot = 2 * (last - 1) + (0 if way > 0 else 1)
+
+                @pl.when(here >= 1)
+                def _(way=way, slot=slot):
+                    self.hop(last, way, p.col).wait_recv()
+                    self.total[...] += self.from_col[slot].astype(F32)
+
+        self.out_copy().start()
+
+    def drain(self):
+        for at, m in enumerate(self.place.members):
+            for copy in self.pair_copies(at, m):
+                copy.wait_send()
+        for at in range(len(self.moves)):
+            self.plane_copy(at).wait_send()
+        for step in range(1, self.place.cols):
+            self.hops(step, lambda c: c.wait_send())
+        self.out_copy().wait()
+
+
+class Swap:
+    def __init__(self, place, links, pieces):
+        self.place, self.links, self.pieces = place, links, pieces
+        self.at = links.take(len(pieces))
+
+    def each(self, act):
+        for i, (source, target) in enumerate(self.pieces):
+            at = self.at + i
+            act(self.links.copy(source, target, self.place.partner, at, at))
+
+    def start(self):
+        self.each(lambda c: c.start())
+
+    def arrive(self):
+        self.each(lambda c: c.wait_recv())
+
+    def drain(self):
+        self.each(lambda c: c.wait_send())
+
+
+class Total:
+    def __init__(self, place, links, sums, arrived, col_first):
+        self.place, self.links, self.sums, self.arrived = place, links, sums, arrived
+        self.col_at = links.take(place.cols - 1)
+        self.row_at = links.take(len(place.row_bits))
+        self.steps = len(place.row_bits) + 1
+        self.col_step = 0 if col_first else self.steps - 1
+
+    def copies(self, i):
+        p = self.place
+        if i == self.col_step:
+            out = []
             for k in range(1, p.cols):
-                far = flipped(p.col, bits_of(k))
-                self.along.append(
-                    self.links.start(self.sums.at[0, far], self.from_col.at[k - 1], (p.row, far))
-                )
-
-    def finish(self):
-        p = self.place
-        total = self.sums[0, p.col].astype(F32)
-        for k in range(1, p.cols):
-            self.along[k - 1].wait_recv()
-            total = total + self.from_col[k - 1].astype(F32)
-        self.out[...] = total
-
-
-class Total:
-    def __init__(self, place, links, sums, arrived):
-        self.place, self.links, self.sums, self.arrived = place, links, sums, arrived
-        self.steps = [(b, 0) for b in place.row_bits] + [(b, 1) for b in bits_of(place.cols - 1)]
-        self.at = 0
-
-    def start(self):
-        p = self.place
-        bit, axis = self.steps[self.at]
-        device = (flipped(p.row, [bit]), p.col) if axis == 0 else (p.row, flipped(p.col, [bit]))
-        self.copy = self.links.start(self.sums.at[self.at % 2], self.arrived.at[self.at], device)
-
-    def step(self):
-        if self.at < len(self.steps):
-            self.copy.wait_recv()
-            if self.at:
-                self.before.wait_send()
-                self.links.open = [c for c in self.links.open if c is not self.before]
-            self.before = self.copy
-            at = self.at
-            self.sums[(at + 1) % 2] = self.sums[at % 2] + self.arrived[at]
-            self.at += 1
-            if self.at < len(self.steps):
-                self.start()
-
-    def finish(self):
-        while self.at < len(self.steps):
-            self.step()
-        return self.sums[self.at % 2]
+                at = self.col_at + k - 1
+                device = (p.row, flipped(p.col, bits_of(k)))
+                into = self.arrived.at[self.steps - 2 + k]
+                out.append(self.links.copy(self.sums.at[i], into, device, at, at))
+            return out
+        bit = i - 1 if self.col_step == 0 else i
+        at = self.row_at + bit
+        device = (flipped(p.row, [p.row_bits[bit]]), p.col)
+        return [self.links.copy(self.sums.at[i], self.arrived.at[bit], device, at, at)]
+
+    def start(self, i=0):
+        for copy in self.copies(i):
+            copy.start()
+
+    def step(self, i):
+        p = self.place
+        for copy in self.copies(i):
+            copy.wait_recv()
+        if i == self.col_step:
+            total = None
+            for c in range(p.cols):
+                term = jnp.where(p.col == c, self.sums[i], 0.0)
+                for k in range(1, p.cols):
+                    here = flipped(p.col, bits_of(k)) == c
+                    term = jnp.where(here, self.arrived[self.steps - 2 + k], term)
+                total = term if total is None else total + term
+        else:
+            total = self.sums[i] + self.arrived[i - 1 if self.col_step == 0 else i]
+        self.sums[i + 1] = total
+        if i + 1 < self.steps:
+            self.start(i + 1)
+
+    def result(self):
+        return self.sums[self.steps]
+
+    def drain(self):
+        for i in range(self.steps):
+            for copy in self.copies(i):
+                copy.wait_send()
 
 
 def flat_rows(value):
@@ -595,88 +826,144 @@
     x_in = Inbound(p, links, g.tokens, g.x)
     e_in = Inbound(p, links, g.encoded, g.e)
     og_in = Inbound(p, links, g.og_low, g.og)
-    x_in.start()
     g.pack_self[:, 0:PAIR] = g.self_query[...]
     g.pack_self[:, PAIR : 2 * PAIR] = g.self_key[...]
     g.pack_self[:, 2 * PAIR :] = g.self_value[...]
-    get_self = Gather(p, links, g.pack_self, g.w_self)
+    get_self = Gather(p, links, g.pack_self, g.w_self, False)
     get_self.start()
+    get_self.start_plane()
+    x_in.start()
     for i, shard in enumerate(
         (g.self_output, g.cross_query, g.cross_key, g.cross_value, g.cross_output)
     ):
-        value = shard[...]
-        if i in (0, 4):
-            value = jnp.transpose(value.astype(F32)).astype(BF16)
-        g.pack_attn[:, i * PAIR : (i + 1) * PAIR] = value
-    get_attn = Gather(p, links, g.pack_attn, g.w_attn)
+        g.pack_attn[:, i * PAIR : (i + 1) * PAIR] = shard[...]
+    get_attn = Gather(p, links, g.pack_attn, g.w_attn, False)
     g.pack_hidden[:, 0:hid] = g.expand[...]
-    g.pack_hidden[:, hid:] = jnp.transpose(g.contract[...].astype(F32)).astype(BF16)
-    get_hidden = Gather(p, links, g.pack_hidden, g.w_hidden)
+    g.pack_hidden[:, hid:] = g.contract[...]
+    get_hidden = Gather(p, links, g.pack_hidden, g.w_hidden, True)
     for m in range(2):
-        g.len_own[m] = jnp.full(g.len_own.shape[1:], g.source_len[m, 0], jnp.int32)
-    len_copy = links.start(g.len_own, g.len_other, p.partner)
+        g.len_own[m] = jnp.full(g.len_own.shape[1:], g.source_len[0, m], jnp.int32)
+    len_swap = Swap(p, links, [(g.len_own, g.len_other)])
+    len_swap.start()
+    levels = range(2, len(p.plane_bits) + 1)
+    get_self.step(1)
+    get_self.plane(0, 1)
+    get_self.step(2)
+    get_self.plane(1, 1)
+    get_self.step(3)
+    get_self.to_pair(0)
+    get_self.plane(2, 1)
+    get_self.plane(3, 1)
+    get_self.to_pair(1)
+    get_attn.start_plane()
     g.og_low[...] = g.out_grad[...].astype(BF16)
-    get_self.after_col()
+    for level in levels:
+        for step in range(cols):
+            get_self.plane(step, level)
+        get_self.to_pair(level)
     get_attn.start()
-    e_in.start()
-    get_self.after_planes()
-    get_attn.after_col()
+    get_hidden.start()
     get_self.finish()
     x_in.arrive()
-
+    e_in.start()
+
+    def key_swap(ref, pairs):
+        pieces = []
+        for at in (low_at, high_at):
+            piece = ref.at[:, pl.ds(pairs[0], pairs[1] - pairs[0]), pl.ds(at, part), :]
+            pieces.append((piece, piece))
+        return Swap(p, links, pieces)
+
+    def keep_keys(ref, z, k_rows, v_rows):
+        for i, value in enumerate((k_rows, v_rows)):
+            ref[i, z, pl.ds(low_at, part), :] = value[:part].astype(BF16)
+            ref[i, z, pl.ds(high_at, part), :] = value[part:].astype(BF16)
+
+    ranges = ((0, cols // 2), (cols // 2, cols))
+    half = cols // 2
+    kv_swaps = [key_swap(g.kv, pairs) for pairs in ranges]
+    ckv_swaps = [key_swap(g.ckv, pairs) for pairs in ranges]
     x = g.x[...]
-    for z in range(cols):
-        rows = dot_nn(x, self_w(z))
-        g.q[z] = ((rows[:, 0:PAIR] + heads_of(g.self_query_bias, z)) * scale).astype(BF16)
-        k_rows = rows[:, PAIR : 2 * PAIR].astype(BF16)
-        v_rows = (rows[:, 2 * PAIR :] + heads_of(g.self_value_bias, z)).astype(BF16)
-        for i, value in enumerate((k_rows, v_rows)):
-            g.kv[i, z, pl.ds(low_at, part), :] = value[:part]
-            g.kv[i, z, pl.ds(high_at, part), :] = value[part:]
-
-    def swap(ref):
-        out = []
-        for at in (low_at, high_at):
-            piece = ref.at[:, :, pl.ds(at, part), :]
-            out.append(links.start(piece, piece, p.partner))
-        return out
-
-    def swapped(copies):
-        for copy in copies:
-            copy.wait_recv()
-
-    kv_swap = swap(g.kv)
-    get_hidden.start()
-    get_attn.after_plane(1)
-    swapped(kv_swap)
-    for block in range(2):
-        for parity in range(2):
-
-            @pl.when(p.core == parity)
-            def _():
-                keys = (4 - parity if block else parity + 1) * part
-                attend_block(
-                    g.q, g.kv, g.mixed, g.lse, block * part, part, keys, causal_last(part, keys)
-                )
-
-        if block == 0:
-            for level in range(2, len(p.plane_bits) + 1):
-                get_attn.after_plane(level)
-            get_hidden.after_col()
-            og_in.start()
+    for pairs, swap in zip(ranges, kv_swaps):
+        for z in range(*pairs):
+            rows = dot_nn(x, self_w(z))
+            g.q[z] = ((rows[:, 0:PAIR] + heads_of(g.self_query_bias, z)) * scale).astype(BF16)
+            keep_keys(
+                g.kv,
+                z,
+                rows[:, PAIR : 2 * PAIR],
+                rows[:, 2 * PAIR :] + heads_of(g.self_value_bias, z),
+            )
+        swap.start()
+
+    def in_segments(work, breaks):
+        def segment(at, carry):
+            block, first = at % 2, (at // 2) * half
+            for i, (before, _) in enumerate(breaks):
+                if before is not None:
+                    pl.when(at == i)(before)
+            work(block, (first, first + half))
+            for i, (_, after) in enumerate(breaks):
+                if after is not None:
+                    pl.when(at == i)(after)
+            return carry
+
+        lax.fori_loop(0, 4, segment, 0)
+
+    def causal_blocks(block, run):
+        for later in range(2):
+            for parity in range(2):
+                keys = (4 - parity if later else parity + 1) * part
+
+                @pl.when(jnp.logical_and(block == later, p.core == parity))
+                def _(later=later, keys=keys):
+                    run(later * part, keys)
+
+    def self_block(block, pairs):
+        causal_blocks(
+            block,
+            lambda row0, keys: attend_block(
+                g.q, g.kv, g.mixed, g.lse, row0, part, keys, causal_last(part, keys), pairs
+            ),
+        )
+
+    def after_self_0():
+        get_attn.step(1)
+        get_attn.plane(0, 1)
+
+    def after_self_1():
+        get_attn.step(2)
+        get_attn.step(3)
+        get_attn.to_pair(0)
+        get_attn.plane(1, 1)
+        for level in levels:
+            get_attn.plane(0, level)
+        get_hidden.step(1)
+        kv_swaps[1].arrive()
+
+    def after_self_2():
+        get_attn.plane(2, 1)
+        get_attn.plane(3, 1)
+        get_attn.to_pair(1)
+        for level in levels:
+            get_attn.plane(1, level)
+        get_hidden.start_plane()
+
+    in_segments(
+        self_block,
+        (
+            (kv_swaps[0].arrive, after_self_0),
+            (None, after_self_1),
+            (None, after_self_2),
+            (None, None),
+        ),
+    )
+    for level in levels:
+        for step in range(2, cols):
+            get_attn.plane(step, level)
+        get_attn.to_pair(level)
+    get_hidden.step(2)
     get_attn.finish()
-    e_in.arrive()
-    len_copy.wait_recv()
-    e = g.e[...]
-    for z in range(cols):
-        rows = dot_nn(e, attn_w(z, 2, 2))
-        k_rows = rows[:, :PAIR].astype(BF16)
-        v_rows = (rows[:, PAIR:] + heads_of(g.cross_value_bias, z)).astype(BF16)
-        for i, value in enumerate((k_rows, v_rows)):
-            g.ckv[i, z, pl.ds(low_at, part), :] = value[:part]
-            g.ckv[i, z, pl.ds(high_at, part), :] = value[part:]
-    ckv_swap = swap(g.ckv)
-
     branch = g.self_output_bias[...] + g.x[...].astype(F32)
     for z in range(cols):
         branch = branch + dot_nt(g.mixed[z], attn_w(z, 0))
@@ -688,7 +975,18 @@
         g.cq[z] = (
             (dot_nn(first_low, attn_w(z, 1)) + heads_of(g.cross_query_bias, z)) * scale
         ).astype(BF16)
-    get_hidden.after_plane(1)
+    e_in.arrive()
+    len_swap.arrive()
+    e = g.e[...]
+    for pairs, swap in zip(ranges, ckv_swaps):
+        for z in range(*pairs):
+            rows = dot_nn(e, attn_w(z, 2, 2))
+            keep_keys(
+                g.ckv, z, rows[:, :PAIR], rows[:, PAIR:] + heads_of(g.cross_value_bias, z)
+            )
+        swap.start()
+    get_hidden.plane(0, 1)
+    get_hidden.plane(1, 1)
 
     mine = p.col % 2 == p.core
     first_micro = p.col // 2 == 0
@@ -704,12 +1002,38 @@
         key = lax.broadcasted_iota(jnp.int32, scores.shape, 0) + at
         return jnp.where(key < limit, scores, NEGATIVE)
 
-    swapped(ckv_swap)
-    for block in range(2):
-        attend_block(g.cq, g.ckv, g.cmixed, g.clse, block * part, part, span, source_mask)
-        if block == 0:
-            for level in range(2, len(p.plane_bits) + 1):
-                get_hidden.after_plane(level)
+    def cross_block(block, pairs):
+        row0 = pl.multiple_of(block * part, part)
+        attend_block(g.cq, g.ckv, g.cmixed, g.clse, row0, part, span, source_mask, pairs)
+
+    def after_cross_0():
+        get_hidden.step(3)
+        get_hidden.to_pair(0)
+        get_hidden.planes_from(0, 2)
+        og_in.start()
+
+    def after_cross_1():
+        get_hidden.plane(2, 1)
+        get_hidden.planes_from(1, 2)
+        ckv_swaps[1].arrive()
+
+    def after_cross_2():
+        get_hidden.plane(3, 1)
+        get_hidden.to_pair(1)
+        get_hidden.planes_from(2, 2)
+
+    in_segments(
+        cross_block,
+        (
+            (ckv_swaps[0].arrive, after_cross_0),
+            (None, after_cross_1),
+            (None, after_cross_2),
+            (None, None),
+        ),
+    )
+    get_hidden.planes_from(3, 2)
+    for level in levels:
+        get_hidden.to_pair(level)
     branch = g.n1[...] * g.attn_gain[...] + g.attn_shift[...] + g.cross_output_bias[...]
     for z in range(cols):
         branch = branch + dot_nt(g.cmixed[z], attn_w(z, 4))
@@ -720,6 +1044,9 @@
     og_in.arrive()
 
     result_out = Outbound(p, links, g.result_low, g.result_home)
+    put_hidden = Reduce(
+        p, links, g.g_hidden, g.p_hidden, g.q_hidden, g.c_hidden, g.t_hidden, g.r_hidden, True
+    )
 
     def hidden_stage(inner_ref, hidden_ref, low_ref, total_ref):
         second = g.n2[...] * g.cross_gain[...] + g.cross_shift[...]
@@ -755,6 +1082,7 @@
             inner_back = (hidden_back * logistic * (1.0 + inner * (1.0 - logistic))).astype(BF16)
             g.small[0, pl.ds(13 + z, 1), :] = column_sum(inner_back.astype(F32))
             g.g_hidden[z, :, :, :hid] = row_blocks(dot_tn(low_ref[...], inner_back), row_count)
+            put_hidden.start_column(z)
             total_ref[...] += dot_nt(inner_back, flat_rows(g.w_hidden[z, :, :, :hid]))
             return carry
 
@@ -774,19 +1102,35 @@
         pltpu.VMEM((own, width), BF16),
         pltpu.VMEM((own, width), F32),
     )
-    put_hidden = Reduce(p, links, g.g_hidden, g.p_hidden, g.q_hidden, g.c_hidden, g.r_hidden)
-    put_hidden.start()
-    put_back = Reduce(p, links, g.g_back, g.p_back, g.q_back, g.c_back, g.r_back)
-    put_enc = Reduce(p, links, g.g_enc, g.p_enc, g.q_enc, g.c_enc, g.r_enc)
-    put_self = Reduce(p, links, g.g_self, g.p_self, g.q_self, g.c_self, g.r_self)
+    put_attn = Reduce(
+        p, links, g.g_attn, g.p_attn, g.q_attn, g.c_attn, g.t_attn, g.r_attn, True
+    )
+    put_self = Reduce(
+        p, links, g.g_self, g.p_self, g.q_self, g.c_self, g.t_self, g.r_self, False
+    )
     enc_out = Outbound(p, links, g.enc_low, g.enc_home)
     tok_out = Outbound(p, links, g.tok_low, g.tok_home)
-
-    def trade(acc_ref, stage_ref, arrive_ref):
+    early = Total(p, links, g.small, g.small_arrived, True)
+    late = Total(p, links, g.late, g.late_arrived, False)
+
+    def trade(stage_ref, arrive_ref, pairs):
+        here = pl.ds(pairs[0], pairs[1] - pairs[0])
+        return Swap(p, links, [(stage_ref.at[:, here], arrive_ref.at[:, here])])
+
+    ckv_trades = [trade(g.stage_cross, g.arrive_cross, pairs) for pairs in ranges]
+    kv_trades = [trade(g.stage_self, g.arrive_self, pairs) for pairs in ranges]
+
+    def hand_over(acc_ref, stage_ref, trades, at):
+        first = ranges[at][0]
+        here = pl.ds(first, half)
         for i in range(2):
-            stage_ref[i, :, 0:part, :] = acc_ref[i, :, pl.ds(other_low, part), :].astype(BF16)
-            stage_ref[i, :, part:own, :] = acc_ref[i, :, pl.ds(other_high, part), :].astype(BF16)
-        return links.start(stage_ref, arrive_ref, p.partner)
+            stage_ref[i, here, 0:part, :] = acc_ref[i, here, pl.ds(other_low, part), :].astype(
+                BF16
+            )
+            stage_ref[i, here, part:own, :] = acc_ref[i, here, pl.ds(other_high, part), :].astype(
+                BF16
+            )
+        trades[at].start()
 
     def joined(acc_ref, arrive_ref, i, z):
         mine_rows = jnp.concatenate(
@@ -798,10 +1142,11 @@
     def back_stage(cross_acc, self_acc):
         grad_low = g.grad[...].astype(BF16)
         for z in range(cols):
-            g.g_back[z, :, :, 2 * PAIR :] = row_blocks(dot_tn(grad_low, g.cmixed[z]), row_count)
+            g.g_attn[z, :, :, 2 * PAIR : 3 * PAIR] = row_blocks(dot_tn(grad_low, g.cmixed[z]), row_count)
             g.mixed_back[z] = dot_nn(grad_low, attn_w(z, 4)).astype(BF16)
         cross_acc[...] = jnp.zeros_like(cross_acc)
-        for block in range(2):
+
+        def cross_block_back(block, pairs):
             attend_block_back(
                 g.cq,
                 g.ckv,
@@ -810,22 +1155,29 @@
                 g.mixed_back,
                 g.dq,
                 cross_acc,
-                block * part,
+                pl.multiple_of(block * part, part),
                 part,
                 span,
                 own,
                 source_mask_back,
+                pairs,
             )
-            if block == 0:
-                put_hidden.after_pair()
-        ckv_trade = trade(cross_acc, g.stage_cross, g.arrive_cross)
+
+        def after_back_1():
+            hand_over(cross_acc, g.stage_cross, ckv_trades, 0)
+
+        in_segments(
+            cross_block_back,
+            ((put_hidden.after_pair, None), (None, after_back_1), (None, None), (None, None)),
+        )
+        hand_over(cross_acc, g.stage_cross, ckv_trades, 1)
         put_hidden.after_plane(0)
         normed = g.n1[...]
         first_low = (normed * g.attn_gain[...] + g.attn_shift[...]).astype(BF16)
         gradient = g.grad[...]
         for z in range(cols):
             dq = g.dq[z]
-            g.g_back[z, :, :, PAIR : 2 * PAIR] = row_blocks(dot_tn(first_low, dq), row_count)
+            g.g_attn[z, :, :, PAIR : 2 * PAIR] = row_blocks(dot_tn(first_low, dq), row_count)
             g.small[0, 11:12, z * PAIR : (z + 1) * PAIR] = column_sum(dq.astype(F32))
             gradient = gradient + dot_nt(dq, attn_w(z, 1))
         g.small[0, 6:7, :] = column_sum(gradient * normed)
@@ -835,90 +1187,128 @@
         g.grad[...] = first_grad
         grad_low = first_grad.astype(BF16)
         for z in range(cols):
-            g.g_back[z, :, :, 0:PAIR] = row_blocks(dot_tn(grad_low, g.mixed[z]), row_count)
+            g.g_attn[z, :, :, 0:PAIR] = row_blocks(dot_tn(grad_low, g.mixed[z]), row_count)
             g.mixed_back[z] = dot_nn(grad_low, attn_w(z, 0)).astype(BF16)
-        put_back.start()
-
-        ckv_trade.wait_recv()
+
+        early.start()
+
+        for swap in ckv_trades:
+            swap.arrive()
         e = g.e[...]
         for z in range(cols):
             dk = joined(cross_acc, g.arrive_cross, 0, z)
             dv = joined(cross_acc, g.arrive_cross, 1, z)
-            g.small[0, 12:13, z * PAIR : (z + 1) * PAIR] = column_sum(dv.astype(F32))
+            g.late[0, 2:3, z * PAIR : (z + 1) * PAIR] = column_sum(dv.astype(F32))
             both = jnp.concatenate([dk, dv], axis=1)
-            g.g_enc[z] = row_blocks(dot_tn(e, both), row_count)
+            g.g_attn[z, :, :, 3 * PAIR :] = row_blocks(dot_tn(e, both), row_count)
+            put_attn.start_column(z)
             term = dot_nt(both, attn_w(z, 2, 2))
             total = term if z == 0 else total + term
         g.enc_low[...] = total.astype(BF16)
         enc_out.start()
-        put_enc.start()
+
+        self_acc[...] = jnp.zeros_like(self_acc)
+
+        def self_block_back(block, pairs):
+            causal_blocks(
+                block,
+                lambda row0, keys: attend_block_back(
+                    g.q,
+                    g.kv,
+                    g.mixed,
+                    g.lse,
+                    g.mixed_back,
+                    g.dq,
+                    self_acc,
+                    row0,
+                    part,
+                    keys,
+                    part,
+                    causal_last_back(part, keys),
+                    pairs,
+                ),
+            )
+
+
         for level in range(1, len(p.plane_bits)):
             put_hidden.after_plane(level)
 
-        self_acc[...] = jnp.zeros_like(self_acc)
-        for block in range(2):
-            for parity in range(2):
-
-                @pl.when(p.core == parity)
-                def _():
-                    keys = (4 - parity if block else parity + 1) * part
-                    attend_block_back(
-                        g.q,
-                        g.kv,
-                        g.mixed,
-                        g.lse,
-                        g.mixed_back,
-                        g.dq,
-                        self_acc,
-                        block * part,
-                        part,
-                        keys,
-                        part,
-                        causal_last_back(part, keys),
-                    )
-
-            if block == 0:
-                put_back.after_pair()
-                put_enc.after_pair()
-        kv_trade = trade(self_acc, g.stage_self, g.arrive_self)
-        for level in range(len(p.plane_bits)):
-            put_back.after_plane(level)
-            put_enc.after_plane(level)
-        kv_trade.wait_recv()
+        def after_back_0():
+            put_attn.after_pair()
+            early.step(0)
+
+        def after_back_1():
+            hand_over(self_acc, g.stage_self, kv_trades, 0)
+            put_hidden.step(1)
+            early.step(1)
+
+        def after_back_2():
+            put_attn.after_plane(0)
+            early.step(2)
+
+        in_segments(
+            self_block_back,
+            ((None, after_back_0), (None, after_back_1), (None, after_back_2), (None, None)),
+        )
+        hand_over(self_acc, g.stage_self, kv_trades, 1)
+        for level in range(1, len(p.plane_bits)):
+            put_attn.after_plane(level)
+        put_hidden.step(2)
+        for i in range(3, early.steps):
+            early.step(i)
+        for swap in kv_trades:
+            swap.arrive()
         x = g.x[...]
         total = g.grad[...]
         for z in range(cols):
             dq = g.dq[z]
             dk = joined(self_acc, g.arrive_self, 0, z)
             dv = joined(self_acc, g.arrive_self, 1, z)
-            g.small[0, 9:10, z * PAIR : (z + 1) * PAIR] = column_sum(dq.astype(F32))
-            g.small[0, 10:11, z * PAIR : (z + 1) * PAIR] = column_sum(dv.astype(F32))
+            g.late[0, 0:1, z * PAIR : (z + 1) * PAIR] = column_sum(dq.astype(F32))
+            g.late[0, 1:2, z * PAIR : (z + 1) * PAIR] = column_sum(dv.astype(F32))
             both = jnp.concatenate([dq, dk, dv], axis=1)
             g.g_self[z] = row_blocks(dot_tn(x, both), row_count)
             total = total + dot_nt(both, self_w(z))
         g.tok_low[...] = total.astype(BF16)
 
+        put_attn.step(1)
+        late.start()
+        put_self.start()
         tok_out.start()
-        put_self.start()
-        total = Total(p, links, g.small, g.small_arrived)
-        total.start()
-        put_hidden.finish()
-        put_back.finish()
-        put_enc.finish()
         put_self.after_pair()
-        total.step()
-        for level in range(len(p.plane_bits)):
+        put_attn.step(2)
+        late.step(0)
+        put_self.after_plane(0)
+        late.step(1)
+        for level in range(1, len(p.plane_bits)):
             put_self.after_plane(level)
-            total.step()
-        g.r_small[...] = total.finish()
+        for i in range(2, late.steps - 1):
+            late.step(i)
+        put_hidden.finish(2)
+        put_attn.finish(2)
+        late.step(late.steps - 1)
+        g.t_small[...] = early.result()
+        g.t_small[9:11, :] = late.result()[0:2, :]
+        g.t_small[12:13, :] = late.result()[2:3, :]
+        small_out = pltpu.make_async_copy(g.t_small, g.r_small, g.recv.at[small_at])
+        small_out.start()
         put_self.finish()
         for moved in (result_out, enc_out, tok_out):
             moved.arrive()
             moved.drain()
-        for moved in (x_in, e_in, og_in):
+        small_out.wait()
+        for moved in (x_in, e_in, og_in, get_self, get_attn, get_hidden, len_swap, early, late):
             moved.drain()
-        links.drain()
-
+        for moved in kv_swaps + ckv_swaps + ckv_trades + kv_trades:
+            moved.drain()
+        for moved in (put_hidden, put_attn, put_self):
+            moved.drain()
+        assert links.count <= g.send.shape[0]
+
+    small_at = links.take()
+    g.small[0, 9:11, :] = jnp.zeros((2, width), F32)
+    g.small[0, 12:13, :] = jnp.zeros((1, width), F32)
+    g.late[0] = jnp.zeros(g.late.shape[1:], F32)
     count = g.small.shape[1]
     g.small[0, 13 + cols : count, :] = jnp.zeros((count - 13 - cols, width), F32)
     pl.run_scoped(
@@ -941,13 +1331,13 @@
     o.self_query[...] = block(g.r_self, 0)
     o.self_key[...] = block(g.r_self, 1)
     o.self_value[...] = block(g.r_self, 2)
-    o.self_output[...] = jnp.transpose(block(g.r_back, 0))
-    o.cross_query[...] = block(g.r_back, 1)
-    o.cross_output[...] = jnp.transpose(block(g.r_back, 2))
-    o.cross_key[...] = block(g.r_enc, 0)
-    o.cross_value[...] = block(g.r_enc, 1)
+    o.self_output[...] = block(g.r_attn, 0)
+    o.cross_query[...] = block(g.r_attn, 1)
+    o.cross_output[...] = block(g.r_attn, 2)
+    o.cross_key[...] = block(g.r_attn, 3)
+    o.cross_value[...] = block(g.r_attn, 4)
     o.expand[...] = g.r_hidden[:, :hid]
-    o.contract[...] = jnp.transpose(g.r_hidden[:, hid:])
+    o.contract[...] = g.r_hidden[:, hid:]
     vectors = (
         o.final_gain,
         o.final_shift,
@@ -1001,6 +1391,10 @@
     final_shift,
 ):
     inputs = dict(locals())
+    names = tuple(inputs)
+    turned = [v is source_len or v is self_output or v is cross_output or v is contract
+              for v in inputs.values()]
+    flat = [v.ndim == 1 for v in inputs.values()]
     row_count = lax.axis_size(ROW)
     cols = lax.axis_size(COL)
     micro_count, part, width = tokens.shape
@@ -1011,10 +1405,11 @@
     own = 2 * part
     plane = row_count // 2
     small_rows = -(-(13 + cols) // 8) * 8
-    small_steps = len(bits_of(row_count - 1)) + len(bits_of(cols - 1))
-    links = 3 * (cols - 1 + 2 * (plane - 1) + 2 * plane)
-    links += 4 * (plane + 2 * (plane - 1) + cols - 1) + small_steps
-    links += 6 * 2 + 1 + 4 + 2
+    row_steps = len(bits_of(row_count - 1))
+    small_steps = row_steps + cols - 1
+    links = 3 * (2 * (cols - 1) + (plane - 1) * cols + plane)
+    links += 3 * (plane + 2 * (plane - 1) + 2 * (cols - 1) + 1) + 2 * plane * (cols - 1)
+    links += 6 * 2 + 1 + 8 + 4 + 2 * small_steps + 1
 
     def whole(columns):
         return pltpu.VMEM((cols, row_count, depth, columns), BF16)
@@ -1026,7 +1421,7 @@
         return pltpu.VMEM((2 * (plane - 1), cols // 2, depth, columns), BF16)
 
     def from_col(columns):
-        return pltpu.VMEM((cols - 1, depth, columns), BF16)
+        return pltpu.VMEM((2 * (cols - 1), depth, columns), BF16)
 
     rows_low = pltpu.VMEM((own, width), BF16)
     rows_f32 = pltpu.VMEM((own, width), F32)
@@ -1071,20 +1466,22 @@
         arrive_cross=half_keys,
         stage_self=half_keys,
         arrive_self=half_keys,
-        small=pltpu.VMEM((2, small_rows, width), F32),
+        small=pltpu.VMEM((row_steps + 2, small_rows, width), F32),
         small_arrived=pltpu.VMEM((small_steps, small_rows, width), F32),
+        late=pltpu.VMEM((row_steps + 2, 8, width), F32),
+        late_arrived=pltpu.VMEM((small_steps, 8, width), F32),
+        t_hidden=pltpu.VMEM((depth, 2 * hid), F32),
+        t_attn=pltpu.VMEM((depth, 5 * PAIR), F32),
+        t_self=pltpu.VMEM((depth, 3 * PAIR), F32),
+        t_small=pltpu.VMEM((small_rows, width), F32),
         g_hidden=whole(2 * hid),
         p_hidden=from_pair(2 * hid),
         q_hidden=from_plane(2 * hid),
         c_hidden=from_col(2 * hid),
-        g_back=whole(3 * PAIR),
-        p_back=from_pair(3 * PAIR),
-        q_back=from_plane(3 * PAIR),
-        c_back=from_col(3 * PAIR),
-        g_enc=whole(2 * PAIR),
-        p_enc=from_pair(2 * PAIR),
-        q_enc=from_plane(2 * PAIR),
-        c_enc=from_col(2 * PAIR),
+        g_attn=whole(5 * PAIR),
+        p_attn=from_pair(5 * PAIR),
+        q_attn=from_plane(5 * PAIR),
+        c_attn=from_col(5 * PAIR),
         g_self=whole(3 * PAIR),
         p_self=from_pair(3 * PAIR),
         q_self=from_plane(3 * PAIR),
@@ -1097,14 +1494,16 @@
         result_home=(home, ANY_SPEC),
         tok_home=(home, ANY_SPEC),
         enc_home=(home, ANY_SPEC),
-        r_self=(jax.ShapeDtypeStruct((depth, 3 * PAIR), F32), VMEM_SPEC),
-        r_back=(jax.ShapeDtypeStruct((depth, 3 * PAIR), F32), VMEM_SPEC),
-        r_enc=(jax.ShapeDtypeStruct((depth, 2 * PAIR), F32), VMEM_SPEC),
-        r_hidden=(jax.ShapeDtypeStruct((depth, 2 * hid), F32), VMEM_SPEC),
-        r_small=(jax.ShapeDtypeStruct((small_rows, width), F32), VMEM_SPEC),
+        r_self=(jax.ShapeDtypeStruct((depth, 3 * PAIR), F32), ANY_SPEC),
+        r_attn=(jax.ShapeDtypeStruct((depth, 5 * PAIR), F32), ANY_SPEC),
+        r_hidden=(jax.ShapeDtypeStruct((depth, 2 * hid), F32), ANY_SPEC),
+        r_small=(jax.ShapeDtypeStruct((small_rows, width), F32), ANY_SPEC),
     )
-    names = tuple(inputs)
     specs = [ANY_SPEC, ANY_SPEC, SMEM_SPEC] + [VMEM_SPEC] * (len(names) - 3)
+    values = [
+        v.reshape(1, -1) if f else (v.T if t else v)
+        for v, f, t in zip(inputs.values(), flat, turned)
+    ]
     moved = pl.pallas_call(
         functools.partial(layer_kernel, row_count, cols, names + tuple(outs) + tuple(scratch)),
         out_shape=[shape for shape, _ in outs.values()],
@@ -1115,20 +1514,20 @@
             collective_id=0, has_side_effects=True, vmem_limit_bytes=VMEM_LIMIT
         ),
         name="layer",
-    )(*(v.reshape(1, -1) if v.ndim == 1 else v for v in inputs.values()))
-    shapes = [(2, part, width)] * 3 + [inputs[n].shape for n in names[4:]]
+    )(*values)
+    shapes = [(2, part, width)] * 3 + [v.shape for v in values[4:]]
     final = pl.pallas_call(
         functools.partial(finish_kernel, width, tuple(outs), names[4:]),
-        out_shape=[
-            jax.ShapeDtypeStruct((1,) + shape if len(shape) == 1 else shape, F32)
-            for shape in shapes
-        ],
+        out_shape=[jax.ShapeDtypeStruct(shape, F32) for shape in shapes],
         in_specs=[VMEM_SPEC] * len(outs),
         out_specs=[VMEM_SPEC] * len(shapes),
         compiler_params=pltpu.CompilerParams(vmem_limit_bytes=VMEM_LIMIT),
         name="finish",
     )(*moved)
-    return tuple(v.reshape(-1) if v.shape[0] == 1 else v for v in final)
+    return tuple(final[:3]) + tuple(
+        v.reshape(-1) if f else (v.T if t else v)
+        for v, f, t in zip(final[3:], flat[4:], turned[4:])
+    )
 
 
 def solution(mesh):

time: 186 us -> 159 us (0.85)
  Pallas kernels: 176 us -> 158 us
  local copies, waits for them, and re-layouts: 8.85 us -> 0 us
    pallas_call x1, Pallas kernels: 172 us -> 155 us  [per_device(): pl.pallas_call(functools.partial(layer_kernel, row_count, cols, names + t...]
    unnamed x11 -> x0, local copies, waits for them, and re-layouts: 8.85 us -> none
where the time goes in v2:
time: 159 us
  Pallas kernels  158 us (99%)
    pallas_call x1, Pallas kernels, per_device(): pl.pallas_call(functools.partial(layer_kernel, row_count, cols, names + t...  155 us
    pallas_call x1, Pallas kernels, per_device(): pl.pallas_call(functools.partial(finish_kernel, width, tuple(outs), names...  3.55 us

profile of v2, /device:TPU:0, one launch (start us, length us, event | category | flops | bytes accessed | tf_op | source)
XLA Modules:
  0.0 159.1 jit_solution(3643985747146621611)
XLA Ops:
  0.7 154.6 %layer.1 = (bf16[2,256,512]{2,1,0:T(8,128)(2,1)}, bf16[2,256,512]{2,1,0:T(8,128)(2,1)}, bf16[2,256,512]{2,1,0:T(8,128)(2,1)}, f32[64,384]{1,0:T(8,128)}, f32[64,...) custom-call(bf16[2,256,512]{2,1,0:T(8,128)(2,1)} %refs_0_.1, bf16[2,256,512]{2,1,0:T(8,128)(2,1)} %refs_1_.1, ...), custom_call_target="tpu_custom_call" | custom-call | tf_op jit(solution)/shard_map/layer/pallas_call | solution.py:1507
  155.3 3.6 %finish.1 = (f32[2,256,512]{2,1,0:T(8,128)}, f32[2,256,512]{2,1,0:T(8,128)}, f32[2,256,512]{2,1,0:T(8,128)}, f32[64,128]{1,0:T(8,128)}, f32[64,128]{1,0:T(8,128)...) custom-call(bf16[2,256,512]{2,1,0:T(8,128)(2,1)} %get-tuple-element., ...), custom_call_target="tpu_custom_call" | custom-call | tf_op jit(solution)/shard_map/finish/pallas_call | solution.py:1519

commit v3 on v2

--- a/solution.py
+++ b/solution.py
@@ -832,7 +832,6 @@
     get_self = Gather(p, links, g.pack_self, g.w_self, False)
     get_self.start()
     get_self.start_plane()
-    x_in.start()
     for i, shard in enumerate(
         (g.self_output, g.cross_query, g.cross_key, g.cross_value, g.cross_output)
     ):
@@ -847,6 +846,7 @@
     len_swap.start()
     levels = range(2, len(p.plane_bits) + 1)
     get_self.step(1)
+    x_in.start()
     get_self.plane(0, 1)
     get_self.step(2)
     get_self.plane(1, 1)
@@ -938,7 +938,6 @@
         get_attn.plane(1, 1)
         for level in levels:
             get_attn.plane(0, level)
-        get_hidden.step(1)
         kv_swaps[1].arrive()
 
     def after_self_2():
@@ -947,6 +946,7 @@
         get_attn.to_pair(1)
         for level in levels:
             get_attn.plane(1, level)
+        get_hidden.step(1)
         get_hidden.start_plane()
 
     in_segments(
@@ -1276,14 +1276,14 @@
         put_self.start()
         tok_out.start()
         put_self.after_pair()
-        put_attn.step(2)
         late.step(0)
+        late.step(1)
         put_self.after_plane(0)
-        late.step(1)
+        for i in range(2, late.steps - 1):
+            late.step(i)
         for level in range(1, len(p.plane_bits)):
             put_self.after_plane(level)
-        for i in range(2, late.steps - 1):
-            late.step(i)
+        put_attn.step(2)
         put_hidden.finish(2)
         put_attn.finish(2)
         late.step(late.steps - 1)

time: 159 us -> 155 us (0.975)
  Pallas kernels: 158 us -> 154 us
    pallas_call x1, Pallas kernels: 155 us -> 150 us  [per_device(): pl.pallas_call(functools.partial(layer_kernel, row_count, cols, names + t...]
where the time goes in v3:
time: 155 us
  Pallas kernels  154 us (99%)
    pallas_call x1, Pallas kernels, per_device(): pl.pallas_call(functools.partial(layer_kernel, row_count, cols, names + t...  150 us
    pallas_call x1, Pallas kernels, per_device(): pl.pallas_call(functools.partial(finish_kernel, width, tuple(outs), names...  3.55 us

profile of v3, /device:TPU:0, one launch (start us, length us, event | category | flops | bytes accessed | tf_op | source)
XLA Modules:
  0.0 154.8 jit_solution(2771014477270741593)
XLA Ops:
  0.7 150.4 %layer.1 = (bf16[2,256,512]{2,1,0:T(8,128)(2,1)}, bf16[2,256,512]{2,1,0:T(8,128)(2,1)}, bf16[2,256,512]{2,1,0:T(8,128)(2,1)}, f32[64,384]{1,0:T(8,128)}, f32[64,...) custom-call(bf16[2,256,512]{2,1,0:T(8,128)(2,1)} %refs_0_.1, bf16[2,256,512]{2,1,0:T(8,128)(2,1)} %refs_1_.1, ...), custom_call_target="tpu_custom_call" | custom-call | tf_op jit(solution)/shard_map/layer/pallas_call | solution.py:1507
  151.0 3.6 %finish.1 = (f32[2,256,512]{2,1,0:T(8,128)}, f32[2,256,512]{2,1,0:T(8,128)}, f32[2,256,512]{2,1,0:T(8,128)}, f32[64,128]{1,0:T(8,128)}, f32[64,128]{1,0:T(8,128)...) custom-call(bf16[2,256,512]{2,1,0:T(8,128)(2,1)} %get-tuple-element., ...), custom_call_target="tpu_custom_call" | custom-call | tf_op jit(solution)/shard_map/finish/pallas_call | solution.py:1519
